TPU v7x, 128 devices: a whole 4x4x4 slice. The times are simulated.
128 devices in a mesh: row: 16 (over z_hi, y, core), col: 8 (over z_lo, x).
Axes of the slice: x: 4, y: 4, z: 4 (z_hi: 2, z_lo: 2; z = z_hi * 2 + z_lo), core: 2. Of those that a mesh axis runs over, the one named last changes fastest.
Arguments:
- edge_tensor: float32 [1024, 16, 1024], P('row'), may hold values from -0.0234375 to 0.0234375
- site_tensor: float32 [16, 16, 16, 16], replicated, may hold values from -0.375 to 0.375
- left_isometry: float32 [1024, 16, 1024], P('row'), may hold values from -0.0234375 to 0.0234375
- right_isometry: float32 [512, 16, 1024], P('col', None, 'row'), may hold values from -0.03125 to 0.03125
- cotangent: float32 [512, 16, 1024], P('col', None, 'row'), may hold values from -96 to 96
Outputs:
- edge_gradient: float32 [1024, 16, 1024], P('row', 'col')
- site_gradient: float32 [16, 16, 16, 16], replicated
- left_gradient: float32 [1024, 16, 1024], P('row', 'col')
- right_gradient: float32 [512, 16, 1024], P('col', 'row')
All inputs are finite; a program needn't handle non-finite values.
Results may differ from a plain program's by a relative error of at most 0.0003.
Values sent between devices are 32-bit elements; how exact they have to be, the bound alone decides.
No kernel may reach another device: no remote copies, remote signals or barrier semaphores. Data moves between devices by JAX's collectives and lax.ppermute only.
A program may use at most 192 MiB of HBM per device.

v0:
```python
import jax
import jax.numpy as jnp
from jax import lax
from jax.sharding import PartitionSpec as P


def on_device(edge_tensor, site_tensor, left_isometry, right_isometry, cotangent):
    highest = lax.Precision.HIGHEST
    block_rows = edge_tensor.shape[0]
    bond_width = site_tensor.shape[0]
    local_cols = right_isometry.shape[0]
    square = bond_width * bond_width
    site_matrix = jnp.transpose(site_tensor, (1, 2, 0, 3)).reshape(square, square)
    right_whole = lax.all_gather(right_isometry, "row", axis=2, tiled=True)
    first_section = jnp.einsum("aeb,cfb->acef", edge_tensor, right_whole, precision=highest)
    first_flat = first_section.reshape(block_rows, local_cols, square)
    second_flat = jnp.dot(first_flat, site_matrix, precision=highest)
    second_section = second_flat.reshape(block_rows, local_cols, bond_width, bond_width)
    cotangent_whole = lax.all_gather(cotangent, "row", axis=2, tiled=True)
    back_second = jnp.einsum("adk,cgk->acdg", left_isometry, cotangent_whole, precision=highest)
    left_terms = jnp.einsum("acdg,cgk->adk", second_section, cotangent_whole, precision=highest)
    back_flat = back_second.reshape(block_rows, local_cols, square)
    back_first = jnp.dot(back_flat, site_matrix.T, precision=highest).reshape(
        block_rows, local_cols, bond_width, bond_width
    )
    site_terms = jnp.dot(
        first_flat.reshape(-1, square).T, back_flat.reshape(-1, square), precision=highest
    )
    edge_terms = jnp.einsum("acef,cfb->aeb", back_first, right_whole, precision=highest)
    right_terms = jnp.einsum("aeb,acef->cfb", edge_tensor, back_first, precision=highest)
    left_gradient, edge_gradient = (
        lax.psum_scatter(left_terms, "col", scatter_dimension=1, tiled=True),
        lax.psum_scatter(edge_terms, "col", scatter_dimension=1, tiled=True),
    )
    right_gradient = lax.psum_scatter(right_terms, "row", scatter_dimension=1, tiled=True)
    site_total = lax.psum(site_terms, ("row", "col"))
    site_gradient = jnp.transpose(
        site_total.reshape(bond_width, bond_width, bond_width, bond_width), (2, 0, 1, 3)
    )
    return (edge_gradient, site_gradient, left_gradient, right_gradient)


def solution(mesh):
    in_specs = (
        P("row", None, None),
        P(),
        P("row", None, None),
        P("col", None, "row"),
        P("col", None, "row"),
    )
    out_specs = (P("row", "col", None), P(), P("row", "col", None), P("col", "row", None))
    return jax.shard_map(
        on_device, mesh=mesh, in_specs=in_specs, out_specs=out_specs, check_vma=False
    )
```

profile of v0, /device:TPU:1, one launch (start us, length us, event | category | flops | bytes accessed | tf_op | source)
XLA Modules:
  0.0 545.9 jit_solution(1836934325128868645)
XLA Ops:
  7.2 0.0 all-gather.3.cloned.1.call-start
  7.2 2.1 copy.35
  9.4 0.0 all-gather.3.cloned.1.call-update
  9.4 0.0 all-gather.5.cloned.1.call-start
  9.4 2.1 copy.40
  11.6 0.0 all-gather.5.cloned.1.call-update
  11.6 0.0 reduce-scatter.8.cloned.1.call-start
  11.7 75.8 %all-gather.3.cloned.1.call-done = f32[64,16,1024]{0,1,2:T(8,128)} async-done(((f32[64,16,64]{0,1,2:T(8,128)}), f32[64,16,1024]{0,1,2:T(8,128)}) %all-gather.3.cloned.1.call-update) | async-done | bytes 4194320 | tf_op jit(solution)/shard_map/all_gather | solution.py:19
  87.5 7.6 %copy.60 = f32[64,16,1024,1]{2,1,3,0:T(8,128)} copy(f32[64,16,1024,1]{0,1,2,3:T(8,128)} %bitcast.78) | data formatting | bytes 8388608 | tf_op jit(solution)/shard_map/all_gather | solution.py:19
  95.1 34.5 %fusion.11 = f32[64,16,64,16]{2,1,3,0:T(8,128)} fusion(f32[64,16,1024,1]{2,1,3,0:T(8,128)} %copy.60, f32[64,16,1024]{2,1,0:T(8,128)} %param.7), kind=kOutput, calls=%fused_computation.11 | convolution fusion | flops 12884901888 | bytes 12582912 | tf_op jit(solution)/shard_map/adk,cgk->acdg/dot_general | solution.py:20
  129.6 0.0 copy-start.3
  129.6 10.7 %copy.61 = f32[64,64,16,16,1]{1,3,2,4,0:T(8,128)} copy(f32[64,64,16,16,1]{0,3,2,1,4:T(8,128)} %bitcast.79) | data formatting | bytes 8388608 | tf_op jit(solution)/shard_map/adk,cgk->acdg/transpose | solution.py:20
  140.3 0.0 copy-done.3
  140.3 0.0 copy-start.2
  140.3 16.0 %convolution_bitcast_fusion = f32[64,64,16,16]{1,3,2,0:T(8,128)S(1)} fusion(f32[64,64,16,16,1]{1,3,2,4,0:T(8,128)} %copy.61, f32[16,16,16,16]{3,2,1,0:T(8,128)S(1)} %copy-done.3), kind=kOutput, calls=%fused_computation.15 | convolution fusion | flops 3221225472 | bytes 8650752 | tf_op jit(solution)/shard_map/dot_general | solution.py:23
  156.4 0.0 copy-start
  156.4 3.2 copy-done
  159.6 0.0 copy-done.2
  159.6 18.0 %fusion.25 = f32[64,16,1024]{2,0,1:T(8,128)} fusion(f32[64,16,1024]{2,1,0:T(8,128)S(1)} %copy-done.2, f32[64,64,16,16]{1,3,2,0:T(8,128)S(1)} %convolution_bitcast_fusion), kind=kOutput, calls=%fused_computation.18 | convolution fusion | flops 12884901888 | bytes 12582912 | tf_op jit(solution)/shard_map/aeb,acef->cfb/dot_general | solution.py:30
  177.6 0.0 reduce-scatter.8.cloned.1.call-update
  177.6 0.4 reduce-scatter.6.cloned.1.call-start
  178.1 2.8 copy.49
  180.9 0.9 reshape.25
  181.8 0.1 copy.50
  182.0 0.0 all-gather.5.cloned.1.call-done
  182.0 8.1 %copy.65 = f32[64,16,1024,1]{2,1,3,0:T(8,128)} copy(f32[64,16,1024,1]{0,1,2,3:T(8,128)} %bitcast.77) | data formatting | bytes 8388608 | tf_op jit(solution)/shard_map/all_gather | solution.py:14
  190.0 34.7 %fusion.8 = f32[64,16,64,16]{2,1,3,0:T(8,128)} fusion(f32[64,16,1024,1]{2,1,3,0:T(8,128)} %copy.65, f32[64,16,1024]{2,1,0:T(8,128)} %param.5), kind=kOutput, calls=%fused_computation.8 | convolution fusion | flops 12884901888 | bytes 12582912 | tf_op jit(solution)/shard_map/aeb,cfb->acef/dot_general | solution.py:15
  224.7 7.4 %copy.66 = f32[64,64,256,1]{2,1,3,0:T(8,128)} copy(f32[64,64,256,1]{0,2,1,3:T(8,128)} %bitcast.81) | data formatting | bytes 8388608 | tf_op jit(solution)/shard_map/reshape | solution.py:16
  232.1 6.8 %copy.53 = f32[64,16,1024]{2,0,1:T(8,128)} copy(f32[64,16,1024]{0,1,2:T(8,128)} %all-gather.3.cloned.1.call-done) | data formatting | bytes 8388608 | tf_op jit(solution)/shard_map/all_gather | solution.py:19
  238.9 0.0 copy-start.1
  238.9 9.6 %fusion.32 = f32[64,64,16,16]{1,2,3,0:T(8,128)S(1)} fusion(f32[64,64,256,1]{2,1,3,0:T(8,128)} %copy.66, f32[16,16,256]{2,1,0:T(8,128)S(1)} %bitcast.85), kind=kOutput, calls=%fused_computation.22 | convolution fusion | flops 3221225472 | bytes 8650752 | tf_op jit(solution)/shard_map/dot_general | solution.py:17
  248.5 0.0 copy-done.1
  248.5 27.6 %fusion.15 = f32[64,16,1024]{2,0,1:T(8,128)} fusion(f32[64,16,1024]{2,0,1:T(8,128)S(1)} %copy-done.1, f32[64,64,16,16]{1,2,3,0:T(8,128)S(1)} %fusion.32), kind=kOutput, calls=%fused_computation.16 | convolution fusion | flops 12884901888 | bytes 12582912 | tf_op jit(solution)/shard_map/acdg,cgk->adk/dot_general | solution.py:21
  276.1 0.0 reduce-scatter.6.cloned.1.call-update
  276.1 0.0 reduce-scatter.4.cloned.1.call-start
  276.2 7.0 %copy.42 = f32[64,16,1024]{2,0,1:T(8,128)} copy(f32[64,16,1024]{0,1,2:T(8,128)} %all-gather.5.cloned.1.call-done) | data formatting | bytes 8388608 | tf_op jit(solution)/shard_map/all_gather | solution.py:14
  283.2 24.5 %fusion.20 = f32[64,16,1024]{2,0,1:T(8,128)} fusion(f32[64,16,1024]{2,0,1:T(8,128)} %copy.42, f32[64,64,16,16]{1,3,2,0:T(8,128)} %copy-done), kind=kOutput, calls=%fused_computation.17 | convolution fusion | flops 12884901888 | bytes 12582912 | tf_op jit(solution)/shard_map/acef,cfb->aeb/dot_general | solution.py:29
  307.7 0.0 reduce-scatter.4.cloned.1.call-update
  307.8 0.0 all-reduce.2.cloned.1.call-start
  307.8 9.9 %copy.46 = f32[64,64,16,16]{1,0,3,2:T(8,128)} copy(f32[64,64,16,16]{0,3,2,1:T(8,128)} %bitcast.82) | data formatting | bytes 8388608 | tf_op jit(solution)/shard_map/aeb,cfb->acef/transpose | solution.py:15
  317.8 7.9 %reshape_reshape.6 = f32[4096,256]{0,1:T(8,128)} reshape(f32[64,64,16,16]{1,0,3,2:T(8,128)} %copy.46) | data formatting | bytes 8388608 | tf_op jit(solution)/shard_map/reshape;reshape | solution.py:27
  325.7 9.7 %copy.47 = f32[64,64,16,16]{1,0,3,2:T(8,128)} copy(f32[64,64,16,16]{0,3,2,1:T(8,128)} %bitcast.80) | data formatting | bytes 8388608 | tf_op jit(solution)/shard_map/adk,cgk->acdg/transpose | solution.py:20
  335.4 8.2 %reshape_reshape.7 = f32[4096,256]{0,1:T(8,128)} reshape(f32[64,64,16,16]{1,0,3,2:T(8,128)} %copy.47) | data formatting | bytes 8388608 | tf_op jit(solution)/shard_map/reshape;reshape | solution.py:27
  343.6 11.5 %fusion.35 = f32[256,256]{1,0:T(8,128)S(1)} fusion(f32[4096,256]{0,1:T(8,128)} %reshape_reshape.6, f32[4096,256]{0,1:T(8,128)} %reshape_reshape.7), kind=kOutput, calls=%fused_computation.25 | convolution fusion | flops 3221225472 | bytes 8650752 | tf_op jit(solution)/shard_map/dot_general | solution.py:26
  355.1 0.6 reshape.23
  355.7 2.0 copy.115
  357.7 0.0 all-reduce.2.cloned.1.call-update
  357.7 0.0 reduce-scatter.8.cloned.1.call-done
  357.8 1.9 copy.59
  359.7 0.0 reduce-scatter.6.cloned.1.call-done
  359.7 2.2 copy.58
  361.9 18.4 %reduce-scatter.4.cloned.1.call-done = f32[64,2,1024]{2,0,1:T(8,128)} async-done(((f32[64,16,1024]{2,0,1:T(8,128)}), f32[64,2,1024]{2,0,1:T(8,128)}) %reduce-scatter.4.cloned.1.call-update) | async-done | bytes 524304 | tf_op jit(solution)/shard_map/reduce_scatter | solution.py:33
  380.4 2.2 copy.57
  382.6 152.9 %all-reduce.2.cloned.1.call-done = f32[16,16,16,16]{3,2,1,0:T(8,128)} async-done(((f32[16,16,16,16]{3,2,1,0:T(8,128)}), f32[16,16,16,16]{3,2,1,0:T(8,128)}) %all-reduce.2.cloned.1.call-update) | async-done | bytes 262160 | tf_op jit(solution)/shard_map/psum | solution.py:36
  535.5 3.1 copy.117
Async XLA Ops:
  7.2 80.3 %all-gather.3.cloned.1.call-start = ((), (), s32[]{:S(2)}) async-start(), calls=%async_computation.3 | async-start | bytes 8912896 | tf_op jit(solution)/shard_map/all_gather | solution.py:19
  9.4 172.6 %all-gather.5.cloned.1.call-start = ((), (), s32[]{:S(2)}) async-start(), calls=%async_computation.4 | async-start | bytes 8912896 | tf_op jit(solution)/shard_map/all_gather | solution.py:14
  11.6 346.1 %reduce-scatter.8.cloned.1.call-start = ((), (), s32[]{:S(2)}) async-start(), calls=%async_computation.8 | async-start | bytes 4456448 | tf_op jit(solution)/shard_map/reduce_scatter | solution.py:35
  129.6 10.7 %copy-start.3 = (f32[16,16,16,16]{3,2,1,0:T(8,128)S(1)}, f32[16,16,16,16]{3,2,1,0:T(8,128)}, u32[]{:S(2)}) copy-start(f32[16,16,16,16]{3,2,1,0:T(8,128)} %param.6) | copy-start | bytes 786436
  140.3 19.3 %copy-start.2 = (f32[64,16,1024]{2,1,0:T(8,128)S(1)}, f32[64,16,1024]{2,1,0:T(8,128)}, u32[]{:S(2)}) copy-start(f32[64,16,1024]{2,1,0:T(8,128)} %param.5) | copy-start | bytes 12582916
  156.4 3.2 copy-start
  177.6 182.1 %reduce-scatter.6.cloned.1.call-start = ((), (), s32[]{:S(2)}) async-start(), calls=%async_computation.7 | async-start | bytes 4718592 | tf_op jit(solution)/shard_map/reduce_scatter | solution.py:32
  238.9 9.6 %copy-start.1 = (f32[64,16,1024]{2,0,1:T(8,128)S(1)}, f32[64,16,1024]{2,0,1:T(8,128)}, u32[]{:S(2)}) copy-start(f32[64,16,1024]{2,0,1:T(8,128)} %copy.53) | copy-start | bytes 12582916
  276.1 104.2 %reduce-scatter.4.cloned.1.call-start = ((), (), s32[]{:S(2)}) async-start(), calls=%async_computation.5 | async-start | bytes 4718592 | tf_op jit(solution)/shard_map/reduce_scatter | solution.py:33
  307.8 227.8 %all-reduce.2.cloned.1.call-start = ((), (), s32[]{:S(2)}) async-start(), calls=%async_computation.6 | async-start | bytes 4194304 | tf_op jit(solution)/shard_map/psum | solution.py:36
Sparse Core Ops, SparseCore 0:
  11.0 76.4 all-gather.2
  90.5 70.4 all-gather.4
  177.7 76.3 reduce-scatter.7
  276.3 49.8 reduce-scatter.5
  328.4 51.8 reduce-scatter.3
  385.6 149.8 all-reduce.1
where the time goes:
time: 555 us; the launch traced here: 546 us
  waiting for transfers between devices  247 us (45%)
  matrix products  176 us (32%)
  local copies, waits for them, and re-layouts  107 us (19%)
  between operations  14.6 us (3%)
    psum x1, waiting for transfers between devices, on_device(): site_total = lax.psum(site_terms, ('row', 'col'))  153 us
    all_gather x1, waiting for transfers between devices, on_device(): cotangent_whole = lax.all_gather(cotangent, 'row', axis=2, tiled=True)  75.8 us
    dot_general x1, matrix products, on_device(): jnp.einsum('aeb,cfb->acef', edge_tensor, right_whole, precision=highest)  34.7 us
    dot_general x1, matrix products, on_device(): jnp.einsum('adk,cgk->acdg', left_isometry, cotangent_whole, precision=hig...  34.5 us
    dot_general x1, matrix products, on_device(): jnp.einsum('acdg,cgk->adk', second_section, cotangent_whole, precision=hi...  27.6 us
    dot_general x1, matrix products, on_device(): jnp.einsum('acef,cfb->aeb', back_first, right_whole, precision=highest)  24.5 us
    transpose x2, local copies, waits for them, and re-layouts, on_device(): jnp.einsum('adk,cgk->acdg', left_isometry, cotangent_whole, precision=hig...  20.4 us
    reduce_scatter x1, waiting for transfers between devices, on_device(): lax.psum_scatter(edge_terms, 'col', scatter_dimension=1, tiled=True)  18.4 us
  transfers between devices with their start and end apart: 6, of which 3 were waited for; matrix products, arithmetic and copies ran while one was open for 50% of the time, Pallas kernels for 0%

commit v1 on v0

v1 whole, which is shorter than its diff:
```python
import functools
import jax
import jax.numpy as jnp
from jax import lax
from jax.experimental import pallas as pl
from jax.experimental.pallas import tpu as pltpu
from jax.sharding import PartitionSpec as P

F32, BF16 = jnp.float32, jnp.bfloat16
NN = (((1,), (0,)), ((), ()))
NT = (((1,), (1,)), ((), ()))
TN = (((0,), (0,)), ((), ()))
PARAMS = pltpu.CompilerParams(vmem_limit_bytes=60 << 20)
ROWS = 256
CHUNKS = 4


def split(value):
    high = value.astype(BF16)
    return high, (value - high.astype(F32)).astype(BF16)


def dot3(left, right, dims):
    dot = functools.partial(lax.dot_general, dimension_numbers=dims, preferred_element_type=F32)
    return dot(left[0], right[0]) + (dot(left[0], right[1]) + dot(left[1], right[0]))


def swap_into(value, high_ref, low_ref):
    lane = lax.broadcasted_iota(jnp.int32, (16, 128), 1)
    for pair in range(8):
        for tile in range(8):
            first = value[32 * pair : 32 * pair + 16, 128 * tile : 128 * tile + 128]
            second = value[32 * pair + 16 : 32 * pair + 32, 128 * tile : 128 * tile + 128]
            even = jnp.where(lane < 64, first, pltpu.roll(second, 64, 1))
            odd = jnp.where(lane < 64, pltpu.roll(first, 64, 1), second)
            columns = slice(128 * pair, 128 * pair + 128)
            for start, part in ((16 * tile, even), (128 + 16 * tile, odd)):
                high, low = split(part)
                high_ref[start : start + 16, columns] = high
                low_ref[start : start + 16, columns] = low


def unswap_into(value, high_ref, low_ref):
    lane = lax.broadcasted_iota(jnp.int32, (16, 128), 1)
    for pair in range(8):
        for tile in range(8):
            columns = slice(128 * pair, 128 * pair + 128)
            even = value[16 * tile : 16 * tile + 16, columns]
            odd = value[128 + 16 * tile : 128 + 16 * tile + 16, columns]
            first = jnp.where(lane < 64, even, pltpu.roll(odd, 64, 1))
            second = jnp.where(lane < 64, pltpu.roll(even, 64, 1), odd)
            columns = slice(128 * tile, 128 * tile + 128)
            for start, part in ((32 * pair, first), (32 * pair + 16, second)):
                high, low = split(part)
                high_ref[start : start + 16, columns] = high
                low_ref[start : start + 16, columns] = low


def assemble(offsets_ref, piece_refs, whole_ref, sems, high_ref, low_ref):
    block = 64
    copies = []
    count = 0
    for piece in piece_refs:
        for part in range(piece.shape[0] // block):
            start = pl.multiple_of(offsets_ref[count], block)
            copies.append(
                pltpu.make_async_copy(
                    piece.at[pl.ds(part * block, block)], whole_ref.at[pl.ds(start, block)], sems.at[count]
                )
            )
            count += 1
    for copy in copies:
        copy.start()
    for copy in copies:
        copy.wait()

    def one(index, carry):
        rows = pl.ds(pl.multiple_of(index * 64, 64), 64)
        high, low = split(whole_ref[rows, :])
        high_ref[rows, :] = high
        low_ref[rows, :] = low
        return carry

    lax.fori_loop(0, 16, one, 0)


def back_kernel(pieces, offsets_ref, *refs):
    piece_refs = refs[:pieces]
    rows_ref, site_ref = refs[pieces : pieces + 2]
    whole_high, whole_low, back_high, back_low, swapped_high, swapped_low, whole, sems = refs[pieces + 2 :]

    @pl.when(pl.program_id(0) == 0)
    def _():
        assemble(offsets_ref, piece_refs, whole, sems, whole_high, whole_low)

    section = dot3(split(rows_ref[...]), (whole_high[...], whole_low[...]), NN)
    swap_into(section, swapped_high, swapped_low)
    mixed = dot3(split(site_ref[...]), (swapped_high[...], swapped_low[...]), NN)
    unswap_into(mixed, back_high, back_low)


def edge_kernel(pieces, offsets_ref, *refs):
    piece_refs = refs[:pieces]
    back_high_ref, back_low_ref = refs[pieces : pieces + 2]
    whole_high, whole_low, edge_ref, whole, sems = refs[pieces + 2 :]

    @pl.when(pl.program_id(0) == 0)
    def _():
        assemble(offsets_ref, piece_refs, whole, sems, whole_high, whole_low)

    terms = dot3((back_high_ref[...], back_low_ref[...]), (whole_high[...], whole_low[...]), NT)
    for a in range(16):
        edge_ref[:, a, :] = terms[16 * a : 16 * a + 16, :]


def left_kernel(
    edge_ref,
    right_high_ref,
    right_low_ref,
    site_matrix_ref,
    swapped_high_ref,
    swapped_low_ref,
    cotangent_high_ref,
    cotangent_low_ref,
    left_ref,
    site_ref,
    first_high,
    first_low,
    second_high,
    second_low,
):
    first = dot3(split(edge_ref[...]), (right_high_ref[...], right_low_ref[...]), NN)
    swap_into(first, first_high, first_low)
    mixed = dot3(split(site_matrix_ref[...]), (first_high[...], first_low[...]), NN)
    unswap_into(mixed, second_high, second_low)
    site = dot3((first_high[...], first_low[...]), (swapped_high_ref[...], swapped_low_ref[...]), NT)

    @pl.when(pl.program_id(0) == 0)
    def _():
        site_ref[...] = site

    @pl.when(pl.program_id(0) > 0)
    def _():
        site_ref[...] += site

    terms = dot3((second_high[...], second_low[...]), (cotangent_high_ref[...], cotangent_low_ref[...]), NT)
    for a in range(16):
        left_ref[:, a, :] = terms[16 * a : 16 * a + 16, :]


def right_kernel(places_ref, back_high_ref, back_low_ref, edge_ref, own_ref, other_ref, turned_high, turned_low, placed):
    @pl.when(pl.program_id(0) == 0)
    def _():
        for chunk in range(CHUNKS):
            rows = slice(chunk * ROWS, (chunk + 1) * ROWS)
            turned_high[:, rows] = back_high_ref[rows, :].T
            turned_low[:, rows] = back_low_ref[rows, :].T

    terms = dot3((turned_high[...], turned_low[...]), split(edge_ref[...]), NN)
    for block in range(16):
        start = pl.multiple_of(places_ref[block], 64)
        placed[pl.ds(start, 64), :] = terms[64 * block : 64 * block + 64, :]
    own_ref[...] = placed[:512, :]
    other_ref[...] = placed[512:, :]


def resident(shape):
    return pl.BlockSpec(shape, lambda *_: (0,) * len(shape))


ANY = pl.BlockSpec(memory_space=pl.ANY)
SQUARE = jax.ShapeDtypeStruct((1024, 1024), BF16)
CHUNK = pl.BlockSpec((ROWS, 1024), lambda i, *_: (i, 0))


def back_call(offsets, pieces, rows, site_matrix):
    return pl.pallas_call(
        functools.partial(back_kernel, len(pieces)),
        out_shape=(SQUARE,) * 6,
        grid_spec=pltpu.PrefetchScalarGridSpec(
            num_scalar_prefetch=1,
            grid=(CHUNKS,),
            in_specs=[ANY] * len(pieces) + [CHUNK, resident((256, 256))],
            out_specs=[resident((1024, 1024))] * 2 + [CHUNK] * 4,
            scratch_shapes=[pltpu.VMEM((1024, 1024), F32), pltpu.SemaphoreType.DMA((16,))],
        ),
        compiler_params=PARAMS,
        name="back",
    )(offsets, *pieces, rows, site_matrix)


def edge_call(offsets, pieces, back_split):
    return pl.pallas_call(
        functools.partial(edge_kernel, len(pieces)),
        out_shape=(SQUARE, SQUARE, jax.ShapeDtypeStruct((16, 64, 1024), F32)),
        grid_spec=pltpu.PrefetchScalarGridSpec(
            num_scalar_prefetch=1,
            grid=(CHUNKS,),
            in_specs=[ANY] * len(pieces) + [CHUNK, CHUNK],
            out_specs=[resident((1024, 1024))] * 2 + [pl.BlockSpec((16, 16, 1024), lambda i, *_: (0, i, 0))],
            scratch_shapes=[pltpu.VMEM((1024, 1024), F32), pltpu.SemaphoreType.DMA((16,))],
        ),
        compiler_params=PARAMS,
        name="edge",
    )(offsets, *pieces, *back_split)


def left_call(edge_rows, right_split, site_matrix, swapped_split, cotangent_split):
    return pl.pallas_call(
        left_kernel,
        out_shape=(jax.ShapeDtypeStruct((16, 64, 1024), F32), jax.ShapeDtypeStruct((256, 256), F32)),
        grid=(CHUNKS,),
        in_specs=[CHUNK]
        + [resident((1024, 1024))] * 2
        + [resident((256, 256))]
        + [CHUNK] * 2
        + [resident((1024, 1024))] * 2,
        out_specs=[pl.BlockSpec((16, 16, 1024), lambda i: (0, i, 0)), resident((256, 256))],
        scratch_shapes=[pltpu.VMEM((ROWS, 1024), BF16)] * 4,
        compiler_params=PARAMS,
        name="left",
    )(edge_rows, *right_split, site_matrix, *swapped_split, *cotangent_split)


def right_call(places, back_split, edge_rows):
    column = lambda rows: pl.BlockSpec((rows, 256), lambda i, *_: (0, i))
    return pl.pallas_call(
        right_kernel,
        out_shape=(jax.ShapeDtypeStruct((512, 1024), F32),) * 2,
        grid_spec=pltpu.PrefetchScalarGridSpec(
            num_scalar_prefetch=1,
            grid=(4,),
            in_specs=[resident((1024, 1024))] * 2 + [column(1024)],
            out_specs=[column(512)] * 2,
            scratch_shapes=[pltpu.VMEM((1024, 1024), BF16)] * 2 + [pltpu.VMEM((1024, 256), F32)],
        ),
        compiler_params=PARAMS,
        name="right",
    )(places, *back_split, edge_rows)


def row_permute(value, z, y, core):
    pairs = []
    for source in range(16):
        there = ((source // 8) ^ z) * 8 + ((source // 2 + y) % 4) * 2 + ((source % 2) ^ core)
        pairs.append((source, there))
    return lax.ppermute(value, "row", pairs)


def col_permute(value, z, x):
    return lax.ppermute(value, "col", [(i, ((i // 4) ^ z) * 4 + (i + x) % 4) for i in range(8)])


def dense(value):
    cols, bond, width = value.shape
    return jnp.transpose(value.reshape(cols, 2, 8, width), (3, 2, 1, 0)).reshape(width, bond * cols)


def take(value, index):
    return lax.dynamic_index_in_dim(value, index, 0, keepdims=False)


def on_device(edge_tensor, site_tensor, left_isometry, right_isometry, cotangent):
    row = lax.axis_index("row").astype(jnp.int32)
    z, y, core = row // 8, row // 2 % 4, row % 2
    edge_rows = edge_tensor.reshape(1024, 1024)
    left_rows = left_isometry.reshape(1024, 1024)
    back_site = jnp.transpose(site_tensor, (2, 1, 3, 0)).reshape(256, 256)
    front_site = jnp.transpose(site_tensor, (3, 0, 2, 1)).reshape(256, 256)

    def offset_of(other_z, steps, other_core):
        return ((z ^ other_z) * 8 + (y - steps) % 4 * 2 + (core ^ other_core)) * 64

    own = dense(cotangent)
    pair = jnp.concatenate([own, row_permute(own, 1, 0, 0)], 0)
    pieces = [pair] + [row_permute(pair, 0, steps, 0) for steps in (1, 3, 2)]
    pieces += [row_permute(piece, 0, 0, 1) for piece in pieces]
    offsets = jnp.stack([offset_of(j, steps, c) for c in (0, 1) for steps in (0, 1, 3, 2) for j in (0, 1)])
    cotangent_high, cotangent_low, *rest = back_call(offsets, pieces, left_rows, back_site)
    back_split, swapped_split = rest[:2], rest[2:]

    own = dense(right_isometry)
    quad = jnp.concatenate([own] + [row_permute(own, 0, steps, 0) for steps in (1, 3, 2)], 0)
    pieces = [quad, row_permute(quad, 1, 0, 0)]
    pieces += [row_permute(piece, 0, 0, 1) for piece in pieces]
    offsets = jnp.stack([offset_of(j, steps, c) for c in (0, 1) for j in (0, 1) for steps in (0, 1, 3, 2)])

    blocks = [(i % 2) * 8 + i // 2 for i in range(16)]
    places = jnp.stack(
        [((b % 2 ^ core) * 8 + (b // 2 % 4 - y) % 4 * 2 + (b // 8 ^ z)) * 64 for b in blocks]
    )
    right_own, right_other = right_call(places, back_split, edge_rows)

    right_high, right_low, edge_terms = edge_call(offsets, pieces, back_split)
    edge_gradient = lax.psum_scatter(edge_terms, "col", scatter_dimension=0, tiled=True)
    left_terms, site_terms = left_call(
        edge_rows, (right_high, right_low), front_site, swapped_split, (cotangent_high, cotangent_low)
    )
    left_gradient = lax.psum_scatter(left_terms, "col", scatter_dimension=0, tiled=True)

    total = (right_own + row_permute(right_other, 0, 0, 1)).reshape(4, 2, 64, 1024)
    total = total[0] + row_permute(total[1], 0, 1, 0) + row_permute(total[3], 0, 3, 0) + row_permute(total[2], 0, 2, 0)
    right_gradient = total[0] + row_permute(total[1], 1, 0, 0)

    part = site_terms.reshape(2, 128, 256)
    part = (take(part, core) + row_permute(take(part, 1 - core), 0, 0, 1)).reshape(2, 64, 256)
    part = (take(part, z) + row_permute(take(part, 1 - z), 1, 0, 0)).reshape(4, 16, 256)
    part = take(part, y) + sum(row_permute(take(part, (y + k) % 4), 0, k, 0) for k in (1, 2, 3))
    part = part + sum(col_permute(part, 0, k) for k in (1, 2, 3))
    part = part + col_permute(part, 1, 0)
    ring = [part] + [row_permute(part, 0, k, 0) for k in (3, 2, 1)]
    part = lax.dynamic_slice_in_dim(jnp.concatenate(ring + ring, 0), (4 - y) % 4 * 16, 64, 0)
    other = row_permute(part, 1, 0, 0)
    part = jnp.where(z == 0, jnp.concatenate([part, other], 0), jnp.concatenate([other, part], 0))
    other = row_permute(part, 0, 0, 1)
    part = jnp.where(core == 0, jnp.concatenate([part, other], 0), jnp.concatenate([other, part], 0))
    site_gradient = jnp.transpose(part.reshape(16, 16, 16, 16), (3, 1, 0, 2))

    return (
        jnp.transpose(edge_gradient, (1, 0, 2)),
        site_gradient,
        jnp.transpose(left_gradient, (1, 0, 2)),
        right_gradient.reshape(64, 1, 1024),
    )


def solution(mesh):
    in_specs = (
        P("row", None, None),
        P(),
        P("row", None, None),
        P("col", None, "row"),
        P("col", None, "row"),
    )
    out_specs = (P("row", "col", None), P(), P("row", "col", None), P("col", "row", None))
    return jax.shard_map(
        on_device, mesh=mesh, in_specs=in_specs, out_specs=out_specs, check_vma=False
    )
```

time: 555 us -> 290 us (0.52); the launches traced: 546 us -> 289 us
  matrix products: 176 us -> 0 us
  waiting for transfers between devices: 247 us -> 122 us
  local copies, waits for them, and re-layouts: 107 us -> 28.9 us
  Pallas kernels: 0 us -> 76.7 us
  starting transfers between devices: 0.65 us -> 45.5 us
    dot_general x8 -> x0, matrix products: 176 us -> none  [the longest x1 34.7 us: on_device(): jnp.einsum('aeb,cfb->acef', edge_tensor, right_whole, precision=highest)]
    psum x1 -> x0, waiting for transfers between devices: 153 us -> none  [on_device(): site_total = lax.psum(site_terms, ('row', 'col'))]
    ppermute x0 -> x33, waiting for transfers between devices: none -> 122 us  [the longest x29 86.8 us: row_permute(): return lax.ppermute(value, 'row', pairs)]
    pallas_call x0 -> x4, Pallas kernels: none -> 76.7 us  [the longest x1 32.1 us: left_call(): pl.pallas_call(left_kernel, out_shape=(jax.ShapeDtypeStruct((16, 64, 1024...]
    all_gather x2 -> x0, waiting for transfers between devices: 75.9 us -> none  [the longest x1 75.8 us: on_device(): cotangent_whole = lax.all_gather(cotangent, 'row', axis=2, tiled=True)]
    ppermute x0 -> x33, starting transfers between devices: none -> 45.2 us  [the longest x29 40.9 us: row_permute(): return lax.ppermute(value, 'row', pairs)]
    all_gather x4 -> x0, local copies, waits for them, and re-layouts: 29.6 us -> none  [the longest x2 15.1 us: on_device(): right_whole = lax.all_gather(right_isometry, 'row', axis=2, tiled=True)]
    transpose x4 -> x2, local copies, waits for them, and re-layouts: 33.1 us -> 5 us  [the longest x1 2.9 us: on_device(): front_site = jnp.transpose(site_tensor, (3, 0, 2, 1)).reshape(256, 256)]
  transfers between devices with their start and end apart: 6 -> 35, of which waited for: 3 -> 18; matrix products, arithmetic and copies ran while one was open for 50% -> 9% of each run, Pallas kernels for 0% -> 22%
where the time goes in v1:
time: 290 us; the launch traced here: 289 us
  waiting for transfers between devices  122 us (42%)
  Pallas kernels  76.7 us (26%)
  starting transfers between devices  45.5 us (16%)
  local copies, waits for them, and re-layouts  28.9 us (10%)
  between operations  14.4 us (5%)
    ppermute x29, waiting for transfers between devices, row_permute(): return lax.ppermute(value, 'row', pairs)  86.8 us
    ppermute x29, starting transfers between devices, row_permute(): return lax.ppermute(value, 'row', pairs)  40.9 us
    ppermute x4, waiting for transfers between devices, col_permute(): lax.ppermute(value, 'col', [(i, (i // 4 ^ z) * 4 + (i + x) % 4) for i in...  34.8 us
    pallas_call x1, Pallas kernels, left_call(): pl.pallas_call(left_kernel, out_shape=(jax.ShapeDtypeStruct((16, 64, 1024...  32.1 us
    pallas_call x1, Pallas kernels, back_call(): pl.pallas_call(functools.partial(back_kernel, len(pieces)), out_shape=(SQ...  17.2 us
    pallas_call x1, Pallas kernels, edge_call(): pl.pallas_call(functools.partial(edge_kernel, len(pieces)), out_shape=(SQ...  14.2 us
    pallas_call x1, Pallas kernels, right_call(): pl.pallas_call(right_kernel, out_shape=(jax.ShapeDtypeStruct((512, 1024),...  13.2 us
    unnamed x25, local copies, waits for them, and re-layouts  10.2 us
  transfers between devices with their start and end apart: 35, of which 18 were waited for; matrix products, arithmetic and copies ran while one was open for 9% of the time, Pallas kernels for 22%

profile of v1, /device:TPU:1, one launch (start us, length us, event | category | flops | bytes accessed | tf_op | source)
XLA Modules:
  0.0 289.4 jit_solution(6047961858886787125)
XLA Ops:
  7.2 1.6 copy.15
  8.8 0.5 reshape.59
  9.3 2.2 collective-permute-start
  11.4 1.5 collective-permute-start.1
  13.0 1.6 collective-permute-start.2
  14.5 0.7 constant_dynamic-update-slice_fusion.3
  15.3 3.5 %collective-permute-done = f32[64,1024]{1,0:T(8,128)S(1)} collective-permute-done((f32[64,1024]{1,0:T(8,128)S(1)}, f32[64,1024]{1,0:T(8,128)S(1)}, u32[]{:S(2)}, u32[]{:S(2)}) %collective-permute-start) | collective-permute-done | bytes 262176 | tf_op jit(solution)/shard_map/ppermute | solution.py:247
  18.8 0.7 constant_dynamic-update-slice_fusion.2
  19.5 0.7 constant_dynamic-update-slice_fusion.1
  20.3 5.1 %collective-permute-done.2 = f32[64,1024]{1,0:T(8,128)S(1)} collective-permute-done((f32[64,1024]{1,0:T(8,128)S(1)}, f32[64,1024]{1,0:T(8,128)S(1)}, u32[]{:S(2)}, u32[]{:S(2)}) %collective-permute-start.2) | collective-permute-done | bytes 262176 | tf_op jit(solution)/shard_map/ppermute | solution.py:247
  25.4 0.7 constant_dynamic-update-slice_fusion.refs_0_
  26.1 3.6 %collective-permute-start.3 = (f32[256,1024]{1,0:T(8,128)}, f32[256,1024]{1,0:T(8,128)}, u32[]{:S(2)}, u32[]{:S(2)}) collective-permute-start(f32[256,1024]{1,0:T(8,128)} %constant_dynamic-update-slice_fusion.refs_0_), channel_id=1, source_target_pairs={{0,64},{8,72},{16,80},{24,88},{32,96},{40,104},{48,112},{56,120},{... | collective-permute-start | bytes 3145736 | tf_op jit(solution)/shard_map/ppermute | solution.py:247
  29.7 0.5 copy.16
  30.3 0.5 reshape.61
  30.8 26.7 %collective-permute-done.6 = f32[64,1024]{1,0:T(8,128)S(1)} collective-permute-done((f32[64,1024]{1,0:T(8,128)S(1)}, f32[64,1024]{1,0:T(8,128)S(1)}, u32[]{:S(2)}, u32[]{:S(2)}) %collective-permute-start.6) | collective-permute-done | bytes 262176 | tf_op jit(solution)/shard_map/ppermute | solution.py:247
  58.0 2.4 collective-permute-start.8
  60.4 2.7 collective-permute-start.10
  63.0 10.1 %collective-permute-done.7.refs_1_ = f32[128,1024]{1,0:T(8,128)S(1)} collective-permute-done((f32[128,1024]{1,0:T(8,128)S(1)}, f32[128,1024]{1,0:T(8,128)S(1)}, u32[]{:S(2)}, u32[]{:S(2)}) %collective-permute-start.7) | collective-permute-done | bytes 524320 | tf_op jit(solution)/shard_map/ppermute | solution.py:247
  73.2 11.3 %collective-permute-start.4 = (f32[256,1024]{1,0:T(8,128)}, f32[256,1024]{1,0:T(8,128)}, u32[]{:S(2)}, u32[]{:S(2)}) collective-permute-start(f32[256,1024]{1,0:T(8,128)} %constant_dynamic-update-slice_fusion.refs_0_), channel_id=1, source_target_pairs={{0,8},{8,0},{16,24},{24,16},{32,40},{40,32},{48,56},{56,48},{64,72... | collective-permute-start | bytes 3145736 | tf_op jit(solution)/shard_map/ppermute | solution.py:247
  84.6 0.4 collective-permute-start.11
  85.1 0.8 copy-done.3
  85.9 0.4 collective-permute-start.13
  86.3 0.7 stack.137.offsets_ref
  87.0 0.7 stack.138.offsets_ref
  87.7 2.1 copy.17
  89.8 3.1 %reshape.63.refs_9_ = f32[256,256]{1,0:T(8,128)} reshape(f32[16,16,16,16]{3,2,1,0:T(8,128)} %copy.17) | data formatting | bytes 524288 | tf_op jit(solution)/shard_map/reshape | solution.py:268
  92.8 17.2 %back.1 = (bf16[1024,1024]{1,0:T(8,128)(2,1)}, bf16[1024,1024]{1,0:T(8,128)(2,1)}, bf16[1024,1024]{1,0:T(8,128)(2,1)}, bf16[1024,1024]{1,0:T(8,128)(2,1)}, bf16[...) custom-call(s32[16]{0:T(128)} %stack.138.offsets_ref, f32[128,1024]{1,0:T(8,128)} %copy-done.1, f32[128,1024]{1,0:T(8,128)} %copy-done.2, ...), custom_call_target="tpu_custom_call" | custom-call | tf_op jit(solution)/shard_map/back/pallas_call | solution.py:177
  110.0 14.2 %edge.1 = (bf16[1024,1024]{1,0:T(8,128)(2,1)}, bf16[1024,1024]{1,0:T(8,128)(2,1)}, f32[16,64,1024]{2,1,0:T(8,128)}) custom-call(s32[16]{0:T(128)} %stack.137.offsets_ref, f32[256,1024]{1,0:T(8,128)} %constant_dynamic-update-slice_fusion.refs_0_, f32[256,1024]{1,0:T(8,128)} %collective-permute-done.3.refs_1_, f32[256,1024]{1,0:T(8,128)} %collective-permute-done.4.refs_2_, ...), custom_call_target="tpu_custom_call" | custom-call | tf_op jit(solution)/shard_map/edge/pallas_call | solution.py:193
  124.6 2.9 %copy.18 = f32[16,16,16,16]{3,2,1,0:T(8,128)} copy(f32[16,16,16,16]{0,2,3,1:T(8,128)S(1)} %bitcast.79) | data formatting | bytes 524288 | tf_op jit(solution)/shard_map/transpose | solution.py:269
  127.4 3.1 %reshape.65.site_matrix_ref = f32[256,256]{1,0:T(8,128)} reshape(f32[16,16,16,16]{3,2,1,0:T(8,128)} %copy.18) | data formatting | bytes 524288 | tf_op jit(solution)/shard_map/reshape | solution.py:269
  130.5 32.1 %left.1 = (f32[16,64,1024]{2,1,0:T(8,128)}, f32[256,256]{1,0:T(8,128)}) custom-call(f32[1024,1024]{1,0:T(8,128)} %bitcast.76, bf16[1024,1024]{1,0:T(8,128)(2,1)} %get-tuple-element.20.right_high_ref, bf16[1024,1024]{1,0:T(8,128)(2,1)} %get-tuple-element.21.right_low_ref, f32[256,256]{1,0:T(8,128)} %reshape.65.site_matrix_ref, ...), custom_call_target="tpu_custom_call" | custom-call | tf_op jit(solution)/shard_map/left/pallas_call | solution.py:209
  162.7 0.6 stack.155.places_ref
  163.4 13.2 %right.1 = (f32[512,1024]{1,0:T(8,128)}, f32[512,1024]{1,0:T(8,128)}) custom-call(s32[16]{0:T(128)} %stack.155.places_ref, bf16[1024,1024]{1,0:T(8,128)(2,1)} %get-tuple-element.17.refs_4_.back_high_ref, bf16[1024,1024]{1,0:T(8,128)(2,1)} %get-tuple-element.18.refs_5_.back_low_ref, f32[1024,1024]{1,0:T(8,128)} %bitcast.77), custom_call_target="tpu_custom_call" | custom-call | tf_op jit(solution)/shard_map/right/pallas_call | solution.py:227
  176.6 0.5 collective-permute-start.14
  177.1 4.0 %collective-permute-done.14 = f32[128,256]{1,0:T(8,128)S(1)} collective-permute-done((f32[128,256]{1,0:T(8,128)S(1)}, f32[128,256]{1,0:T(8,128)S(1)}, u32[]{:S(2)}, u32[]{:S(2)}) %collective-permute-start.14) | collective-permute-done | bytes 131104 | tf_op jit(solution)/shard_map/ppermute | solution.py:247
  181.1 2.7 collective-permute-start.15
  183.9 2.4 collective-permute-done.15
  186.3 2.3 collective-permute-start.18
  188.6 1.3 collective-permute-start.17
  189.9 2.9 %collective-permute-done.16 = f32[16,256]{1,0:T(8,128)S(1)} collective-permute-done((f32[16,256]{1,0:T(8,128)S(1)}, f32[16,256]{1,0:T(8,128)S(1)}, u32[]{:S(2)}, u32[]{:S(2)}) %collective-permute-start.16) | collective-permute-done | bytes 16416 | tf_op jit(solution)/shard_map/ppermute | solution.py:247
  193.1 2.6 collective-permute-start.21
  195.7 1.3 collective-permute-start.20
  197.0 3.5 %collective-permute-done.19 = f32[16,256]{1,0:T(8,128)S(1)} collective-permute-done((f32[16,256]{1,0:T(8,128)S(1)}, f32[16,256]{1,0:T(8,128)S(1)}, u32[]{:S(2)}, u32[]{:S(2)}) %collective-permute-start.19) | collective-permute-done | bytes 16416 | tf_op jit(solution)/shard_map/ppermute | solution.py:251
  200.7 0.5 collective-permute-start.22
  201.1 31.1 %collective-permute-done.22 = f32[16,256]{1,0:T(8,128)S(1)} collective-permute-done((f32[16,256]{1,0:T(8,128)S(1)}, f32[16,256]{1,0:T(8,128)S(1)}, u32[]{:S(2)}, u32[]{:S(2)}) %collective-permute-start.22) | collective-permute-done | bytes 16416 | tf_op jit(solution)/shard_map/ppermute | solution.py:251
  232.3 2.3 collective-permute-start.23
  234.6 0.7 collective-permute-start.24
  235.3 0.6 collective-permute-start.25
  235.9 2.8 collective-permute-done.24
  239.1 2.0 add.450
  241.3 1.5 collective-permute-start.31
  242.8 0.4 collective-permute-start.30
  243.2 1.1 collective-permute-start.29
  244.4 9.8 %collective-permute-done.31 = f32[2,64,1024]{2,1,0:T(8,128)S(1)} collective-permute-done((f32[2,64,1024]{2,1,0:T(8,128)S(1)}, f32[2,64,1024]{2,1,0:T(8,128)S(1)}, u32[]{:S(2)}, u32[]{:S(2)}) %collective-permute-start.31) | collective-permute-done | bytes 524320 | tf_op jit(solution)/shard_map/ppermute | solution.py:247
  254.2 10.8 %collective-permute-done.30 = f32[2,64,1024]{2,1,0:T(8,128)S(1)} collective-permute-done((f32[2,64,1024]{2,1,0:T(8,128)S(1)}, f32[2,64,1024]{2,1,0:T(8,128)S(1)}, u32[]{:S(2)}, u32[]{:S(2)}) %collective-permute-start.30) | collective-permute-done | bytes 524320 | tf_op jit(solution)/shard_map/ppermute | solution.py:247
  265.0 3.0 %collective-permute-done.29 = f32[2,64,1024]{2,1,0:T(8,128)S(1)} collective-permute-done((f32[2,64,1024]{2,1,0:T(8,128)S(1)}, f32[2,64,1024]{2,1,0:T(8,128)S(1)}, u32[]{:S(2)}, u32[]{:S(2)}) %collective-permute-start.29) | collective-permute-done | bytes 524320 | tf_op jit(solution)/shard_map/ppermute | solution.py:247
  268.3 0.6 collective-permute-start.27
  268.9 1.0 collective-permute-done.27
  269.9 0.6 select_n.221
  270.6 2.6 copy.20
  273.2 4.0 %collective-permute-done.32 = f32[64,1024]{1,0:T(8,128)S(1)} collective-permute-done((f32[64,1024]{1,0:T(8,128)S(1)}, f32[64,1024]{1,0:T(8,128)S(1)}, u32[]{:S(2)}, u32[]{:S(2)}) %collective-permute-start.32) | collective-permute-done | bytes 262176 | tf_op jit(solution)/shard_map/ppermute | solution.py:247
  277.2 0.9 reshape.69
  278.1 2.2 copy.19
  280.3 2.2 copy.21
  (69 shorter events, 2.7 us)
Async XLA Ops:
  7.2 22.6 %copy-start.4 = (f32[64,16,64]{2,1,0:T(8,128)S(1)}, f32[64,16,64]{2,1,0:T(8,128)}, u32[]{:S(2)}) copy-start(f32[64,16,64]{2,1,0:T(8,128)} %param.9) | copy-start | bytes 786436
  7.2 270.9 %reduce-scatter.3.cloned.1.call-start = ((), (), s32[]{:S(2)}) async-start(), calls=%async_computation.2 | async-start | bytes 4718592 | tf_op jit(solution)/shard_map/reduce_scatter | solution.py:295
  9.3 9.5 %collective-permute-start = (f32[64,1024]{1,0:T(8,128)S(1)}, f32[64,1024]{1,0:T(8,128)S(1)}, u32[]{:S(2)}, u32[]{:S(2)}) collective-permute-start(f32[64,1024]{1,0:T(8,128)S(1)} %reshape.59), channel_id=1, source_target_pairs={{0,16},{8,24},{16,32},{24,40},{32,48},{40,56},{48,0},{56,8},{64,80... | collective-permute-start | bytes 786440 | tf_op jit(solution)/shard_map/ppermute | solution.py:247
  11.4 8.1 %collective-permute-start.1 = (f32[64,1024]{1,0:T(8,128)S(1)}, f32[64,1024]{1,0:T(8,128)S(1)}, u32[]{:S(2)}, u32[]{:S(2)}) collective-permute-start(f32[64,1024]{1,0:T(8,128)S(1)} %reshape.59), channel_id=1, source_target_pairs={{0,48},{8,56},{16,0},{24,8},{32,16},{40,24},{48,32},{56,40},{64,11... | collective-permute-start | bytes 786440 | tf_op jit(solution)/shard_map/ppermute | solution.py:247
  13.0 12.4 %collective-permute-start.2 = (f32[64,1024]{1,0:T(8,128)S(1)}, f32[64,1024]{1,0:T(8,128)S(1)}, u32[]{:S(2)}, u32[]{:S(2)}) collective-permute-start(f32[64,1024]{1,0:T(8,128)S(1)} %reshape.59), channel_id=1, source_target_pairs={{0,32},{8,40},{16,48},{24,56},{32,0},{40,8},{48,16},{56,24},{64,96... | collective-permute-start | bytes 786440 | tf_op jit(solution)/shard_map/ppermute | solution.py:247
  19.5 68.1 %copy-start = (f32[16,16,16,16]{3,2,1,0:T(8,128)S(1)}, f32[16,16,16,16]{3,2,1,0:T(8,128)}, u32[]{:S(2)}) copy-start(f32[16,16,16,16]{3,2,1,0:T(8,128)} %param.6) | copy-start | bytes 786436
  26.1 58.3 %collective-permute-start.3 = (f32[256,1024]{1,0:T(8,128)}, f32[256,1024]{1,0:T(8,128)}, u32[]{:S(2)}, u32[]{:S(2)}) collective-permute-start(f32[256,1024]{1,0:T(8,128)} %constant_dynamic-update-slice_fusion.refs_0_), channel_id=1, source_target_pairs={{0,64},{8,72},{16,80},{24,88},{32,96},{40,104},{48,112},{56,120},{... | collective-permute-start | bytes 3145736 | tf_op jit(solution)/shard_map/ppermute | solution.py:247
  30.7 26.8 %collective-permute-start.6 = (f32[64,1024]{1,0:T(8,128)S(1)}, f32[64,1024]{1,0:T(8,128)S(1)}, u32[]{:S(2)}, u32[]{:S(2)}) collective-permute-start(f32[64,1024]{1,0:T(8,128)S(1)} %reshape.61), channel_id=1, source_target_pairs={{0,64},{8,72},{16,80},{24,88},{32,96},{40,104},{48,112},{56,120},{... | collective-permute-start | bytes 786440 | tf_op jit(solution)/shard_map/ppermute | solution.py:247
  57.6 32.2 %copy-start.1 = (f32[128,1024]{1,0:T(8,128)}, f32[128,1024]{1,0:T(8,128)S(1)}, u32[]{:S(2)}) copy-start(f32[128,1024]{1,0:T(8,128)S(1)} %constant_dynamic-update-slice_fusion.4.refs_0_) | copy-start | bytes 1572868
  57.6 15.6 %collective-permute-start.7 = (f32[128,1024]{1,0:T(8,128)S(1)}, f32[128,1024]{1,0:T(8,128)S(1)}, u32[]{:S(2)}, u32[]{:S(2)}) collective-permute-start(f32[128,1024]{1,0:T(8,128)S(1)} %constant_dynamic-update-slice_fusion.4.refs_0_), channel_id=1, source_target_pairs={{0,16},{8,24},{16,32},{24,40},{32,48},{40,56},{48,0},{56,8},{64,80... | collective-permute-start | bytes 1572872 | tf_op jit(solution)/shard_map/ppermute | solution.py:247
  58.0 26.6 %collective-permute-start.8 = (f32[128,1024]{1,0:T(8,128)S(1)}, f32[128,1024]{1,0:T(8,128)}, u32[]{:S(2)}, u32[]{:S(2)}) collective-permute-start(f32[128,1024]{1,0:T(8,128)S(1)} %constant_dynamic-update-slice_fusion.4.refs_0_), channel_id=1, source_target_pairs={{0,48},{8,56},{16,0},{24,8},{32,16},{40,24},{48,32},{56,40},{64,11... | collective-permute-start | bytes 1572872 | tf_op jit(solution)/shard_map/ppermute | solution.py:247
  60.4 24.6 %collective-permute-start.9 = (f32[128,1024]{1,0:T(8,128)S(1)}, f32[128,1024]{1,0:T(8,128)}, u32[]{:S(2)}, u32[]{:S(2)}) collective-permute-start(f32[128,1024]{1,0:T(8,128)S(1)} %constant_dynamic-update-slice_fusion.4.refs_0_), channel_id=1, source_target_pairs={{0,32},{8,40},{16,48},{24,56},{32,0},{40,8},{48,16},{56,24},{64,96... | collective-permute-start | bytes 1572872 | tf_op jit(solution)/shard_map/ppermute | solution.py:247
  60.4 24.7 %collective-permute-start.10 = (f32[128,1024]{1,0:T(8,128)S(1)}, f32[128,1024]{1,0:T(8,128)S(1)}, u32[]{:S(2)}, u32[]{:S(2)}) collective-permute-start(f32[128,1024]{1,0:T(8,128)S(1)} %constant_dynamic-update-slice_fusion.4.refs_0_), channel_id=1, source_target_pairs={{0,8},{8,0},{16,24},{24,16},{32,40},{40,32},{48,56},{56,48},{64,72... | collective-permute-start | bytes 1572872 | tf_op jit(solution)/shard_map/ppermute | solution.py:247
  73.2 16.6 %copy-start.2 = (f32[128,1024]{1,0:T(8,128)}, f32[128,1024]{1,0:T(8,128)S(1)}, u32[]{:S(2)}) copy-start(f32[128,1024]{1,0:T(8,128)S(1)} %collective-permute-done.7.refs_1_) | copy-start | bytes 1572868
  73.2 36.8 %collective-permute-start.4 = (f32[256,1024]{1,0:T(8,128)}, f32[256,1024]{1,0:T(8,128)}, u32[]{:S(2)}, u32[]{:S(2)}) collective-permute-start(f32[256,1024]{1,0:T(8,128)} %constant_dynamic-update-slice_fusion.refs_0_), channel_id=1, source_target_pairs={{0,8},{8,0},{16,24},{24,16},{32,40},{40,32},{48,56},{56,48},{64,72... | collective-permute-start | bytes 3145736 | tf_op jit(solution)/shard_map/ppermute | solution.py:247
  84.5 25.6 %collective-permute-start.5 = (f32[256,1024]{1,0:T(8,128)}, f32[256,1024]{1,0:T(8,128)}, u32[]{:S(2)}, u32[]{:S(2)}) collective-permute-start(f32[256,1024]{1,0:T(8,128)} %collective-permute-done.3.refs_1_), channel_id=1, source_target_pairs={{0,8},{8,0},{16,24},{24,16},{32,40},{40,32},{48,56},{56,48},{64,72... | collective-permute-start | bytes 3145736 | tf_op jit(solution)/shard_map/ppermute | solution.py:247
  84.6 8.3 %collective-permute-start.11 = (f32[128,1024]{1,0:T(8,128)S(1)}, f32[128,1024]{1,0:T(8,128)}, u32[]{:S(2)}, u32[]{:S(2)}) collective-permute-start(f32[128,1024]{1,0:T(8,128)S(1)} %collective-permute-done.7.refs_1_), channel_id=1, source_target_pairs={{0,8},{8,0},{16,24},{24,16},{32,40},{40,32},{48,56},{56,48},{64,72... | collective-permute-start | bytes 1572872 | tf_op jit(solution)/shard_map/ppermute | solution.py:247
  85.0 7.8 %collective-permute-start.12 = (f32[128,1024]{1,0:T(8,128)}, f32[128,1024]{1,0:T(8,128)}, u32[]{:S(2)}, u32[]{:S(2)}) collective-permute-start(f32[128,1024]{1,0:T(8,128)} %collective-permute-done.8.refs_2_), channel_id=1, source_target_pairs={{0,8},{8,0},{16,24},{24,16},{32,40},{40,32},{48,56},{56,48},{64,72... | collective-permute-start | bytes 1572872 | tf_op jit(solution)/shard_map/ppermute | solution.py:247
  85.1 0.8 copy-start.3
  85.9 7.0 %collective-permute-start.13 = (f32[128,1024]{1,0:T(8,128)}, f32[128,1024]{1,0:T(8,128)}, u32[]{:S(2)}, u32[]{:S(2)}) collective-permute-start(f32[128,1024]{1,0:T(8,128)} %collective-permute-done.9.refs_3_), channel_id=1, source_target_pairs={{0,8},{8,0},{16,24},{24,16},{32,40},{40,32},{48,56},{56,48},{64,72... | collective-permute-start | bytes 1572872 | tf_op jit(solution)/shard_map/ppermute | solution.py:247
  124.3 156.0 %reduce-scatter.5.cloned.1.call-start = ((), (), s32[]{:S(2)}) async-start(), calls=%async_computation.3 | async-start | bytes 4718592 | tf_op jit(solution)/shard_map/reduce_scatter | solution.py:299
  163.4 13.2 %copy-start.5 = (f32[256,256]{1,0:T(8,128)S(1)}, f32[256,256]{1,0:T(8,128)}, u32[]{:S(2)}) copy-start(f32[256,256]{1,0:T(8,128)} %get-tuple-element.26) | copy-start | bytes 786436
  176.5 62.6 %collective-permute-start.28 = (f32[512,1024]{1,0:T(8,128)}, f32[512,1024]{1,0:T(8,128)S(1)}, u32[]{:S(2)}, u32[]{:S(2)}) collective-permute-start(f32[512,1024]{1,0:T(8,128)} %get-tuple-element.29), channel_id=1, source_target_pairs={{0,8},{8,0},{16,24},{24,16},{32,40},{40,32},{48,56},{56,48},{64,72... | collective-permute-start | bytes 6291464 | tf_op jit(solution)/shard_map/ppermute | solution.py:247
  176.6 4.5 %collective-permute-start.14 = (f32[128,256]{1,0:T(8,128)S(1)}, f32[128,256]{1,0:T(8,128)S(1)}, u32[]{:S(2)}, u32[]{:S(2)}) collective-permute-start(f32[128,256]{1,0:T(8,128)S(1)} %dynamic-slice_bitcast_fusion), channel_id=1, source_target_pairs={{0,8},{8,0},{16,24},{24,16},{32,40},{40,32},{48,56},{56,48},{64,72... | collective-permute-start | bytes 393224 | tf_op jit(solution)/shard_map/ppermute | solution.py:247
  181.1 5.1 %collective-permute-start.15 = (f32[64,256]{1,0:T(8,128)S(1)}, f32[64,256]{1,0:T(8,128)S(1)}, u32[]{:S(2)}, u32[]{:S(2)}) collective-permute-start(f32[64,256]{1,0:T(8,128)S(1)} %dynamic-slice_bitcast_fusion.1), channel_id=1, source_target_pairs={{0,64},{8,72},{16,80},{24,88},{32,96},{40,104},{48,112},{56,120},{... | collective-permute-start | bytes 196616 | tf_op jit(solution)/shard_map/ppermute | solution.py:247
  186.3 3.6 %collective-permute-start.18 = (f32[16,256]{1,0:T(8,128)S(1)}, f32[16,256]{1,0:T(8,128)S(1)}, u32[]{:S(2)}, u32[]{:S(2)}) collective-permute-start(f32[16,256]{1,0:T(8,128)S(1)} %get-tuple-element.45), channel_id=1, source_target_pairs={{0,48},{8,56},{16,0},{24,8},{32,16},{40,24},{48,32},{56,40},{64,11... | collective-permute-start | bytes 49160 | tf_op jit(solution)/shard_map/ppermute | solution.py:247
  188.6 4.2 %collective-permute-start.16 = (f32[16,256]{1,0:T(8,128)S(1)}, f32[16,256]{1,0:T(8,128)S(1)}, u32[]{:S(2)}, u32[]{:S(2)}) collective-permute-start(f32[16,256]{1,0:T(8,128)S(1)} %get-tuple-element.46), channel_id=1, source_target_pairs={{0,16},{8,24},{16,32},{24,40},{32,48},{40,56},{48,0},{56,8},{64,80... | collective-permute-start | bytes 49160 | tf_op jit(solution)/shard_map/ppermute | solution.py:247
  188.6 4.5 %collective-permute-start.17 = (f32[16,256]{1,0:T(8,128)S(1)}, f32[16,256]{1,0:T(8,128)S(1)}, u32[]{:S(2)}, u32[]{:S(2)}) collective-permute-start(f32[16,256]{1,0:T(8,128)S(1)} %get-tuple-element.44), channel_id=1, source_target_pairs={{0,32},{8,40},{16,48},{24,56},{32,0},{40,8},{48,16},{56,24},{64,96... | collective-permute-start | bytes 49160 | tf_op jit(solution)/shard_map/ppermute | solution.py:247
  193.1 3.9 %collective-permute-start.21 = (f32[16,256]{1,0:T(8,128)S(1)}, f32[16,256]{1,0:T(8,128)S(1)}, u32[]{:S(2)}, u32[]{:S(2)}) collective-permute-start(f32[16,256]{1,0:T(8,128)S(1)} %bitcast_add_fusion.2), channel_id=1, source_target_pairs={{0,3},{1,0},{2,1},{3,2},{4,7},{5,4},{6,5},{7,6},{8,11},{9,8},{10,9... | collective-permute-start | bytes 49160 | tf_op jit(solution)/shard_map/ppermute | solution.py:251
  195.7 4.8 %collective-permute-start.19 = (f32[16,256]{1,0:T(8,128)S(1)}, f32[16,256]{1,0:T(8,128)S(1)}, u32[]{:S(2)}, u32[]{:S(2)}) collective-permute-start(f32[16,256]{1,0:T(8,128)S(1)} %bitcast_add_fusion.2), channel_id=1, source_target_pairs={{0,1},{1,2},{2,3},{3,0},{4,5},{5,6},{6,7},{7,4},{8,9},{9,10},{10,1... | collective-permute-start | bytes 49160 | tf_op jit(solution)/shard_map/ppermute | solution.py:251
  195.7 5.0 %collective-permute-start.20 = (f32[16,256]{1,0:T(8,128)S(1)}, f32[16,256]{1,0:T(8,128)S(1)}, u32[]{:S(2)}, u32[]{:S(2)}) collective-permute-start(f32[16,256]{1,0:T(8,128)S(1)} %bitcast_add_fusion.2), channel_id=1, source_target_pairs={{0,2},{1,3},{2,0},{3,1},{4,6},{5,7},{6,4},{7,5},{8,10},{9,11},{10,... | collective-permute-start | bytes 49160 | tf_op jit(solution)/shard_map/ppermute | solution.py:251
  200.7 31.6 %collective-permute-start.22 = (f32[16,256]{1,0:T(8,128)S(1)}, f32[16,256]{1,0:T(8,128)S(1)}, u32[]{:S(2)}, u32[]{:S(2)}) collective-permute-start(f32[16,256]{1,0:T(8,128)S(1)} %add_add_fusion.1), channel_id=1, source_target_pairs={{0,4},{1,5},{2,6},{3,7},{4,0},{5,1},{6,2},{7,3},{8,12},{9,13},{10,... | collective-permute-start | bytes 49160 | tf_op jit(solution)/shard_map/ppermute | solution.py:251
  232.3 3.6 %collective-permute-start.23 = (f32[16,256]{1,0:T(8,128)S(1)}, f32[16,256]{1,0:T(8,128)S(1)}, u32[]{:S(2)}, u32[]{:S(2)}) collective-permute-start(f32[16,256]{1,0:T(8,128)S(1)} %get-tuple-element.39), channel_id=1, source_target_pairs={{0,48},{8,56},{16,0},{24,8},{32,16},{40,24},{48,32},{56,40},{64,11... | collective-permute-start | bytes 49160 | tf_op jit(solution)/shard_map/ppermute | solution.py:247
  234.6 4.1 %collective-permute-start.24 = (f32[16,256]{1,0:T(8,128)S(1)}, f32[16,256]{1,0:T(8,128)S(1)}, u32[]{:S(2)}, u32[]{:S(2)}) collective-permute-start(f32[16,256]{1,0:T(8,128)S(1)} %get-tuple-element.39), channel_id=1, source_target_pairs={{0,32},{8,40},{16,48},{24,56},{32,0},{40,8},{48,16},{56,24},{64,96... | collective-permute-start | bytes 49160 | tf_op jit(solution)/shard_map/ppermute | solution.py:247
  235.3 3.8 %collective-permute-start.25 = (f32[16,256]{1,0:T(8,128)S(1)}, f32[16,256]{1,0:T(8,128)S(1)}, u32[]{:S(2)}, u32[]{:S(2)}) collective-permute-start(f32[16,256]{1,0:T(8,128)S(1)} %get-tuple-element.39), channel_id=1, source_target_pairs={{0,16},{8,24},{16,32},{24,40},{32,48},{40,56},{48,0},{56,8},{64,80... | collective-permute-start | bytes 49160 | tf_op jit(solution)/shard_map/ppermute | solution.py:247
  241.3 12.9 %collective-permute-start.31 = (f32[2,64,1024]{2,1,0:T(8,128)S(1)}, f32[2,64,1024]{2,1,0:T(8,128)S(1)}, u32[]{:S(2)}, u32[]{:S(2)}) collective-permute-start(f32[2,64,1024]{2,1,0:T(8,128)S(1)} %bitcast.93), channel_id=1, source_target_pairs={{0,32},{8,40},{16,48},{24,56},{32,0},{40,8},{48,16},{56,24},{64,96... | collective-permute-start | bytes 1572872 | tf_op jit(solution)/shard_map/ppermute | solution.py:247
  242.8 22.2 %collective-permute-start.30 = (f32[2,64,1024]{2,1,0:T(8,128)S(1)}, f32[2,64,1024]{2,1,0:T(8,128)S(1)}, u32[]{:S(2)}, u32[]{:S(2)}) collective-permute-start(f32[2,64,1024]{2,1,0:T(8,128)S(1)} %bitcast.92), channel_id=1, source_target_pairs={{0,48},{8,56},{16,0},{24,8},{32,16},{40,24},{48,32},{56,40},{64,11... | collective-permute-start | bytes 1572872 | tf_op jit(solution)/shard_map/ppermute | solution.py:247
  243.2 24.8 %collective-permute-start.29 = (f32[2,64,1024]{2,1,0:T(8,128)S(1)}, f32[2,64,1024]{2,1,0:T(8,128)S(1)}, u32[]{:S(2)}, u32[]{:S(2)}) collective-permute-start(f32[2,64,1024]{2,1,0:T(8,128)S(1)} %bitcast.91), channel_id=1, source_target_pairs={{0,16},{8,24},{16,32},{24,40},{32,48},{40,56},{48,0},{56,8},{64,80... | collective-permute-start | bytes 1572872 | tf_op jit(solution)/shard_map/ppermute | solution.py:247
  244.3 24.0 %collective-permute-start.26 = (f32[64,256]{1,0:T(8,128)S(1)}, f32[64,256]{1,0:T(8,128)S(1)}, u32[]{:S(2)}, u32[]{:S(2)}) collective-permute-start(f32[64,256]{1,0:T(8,128)S(1)} %constant_dynamic-slice_fusion), channel_id=1, source_target_pairs={{0,64},{8,72},{16,80},{24,88},{32,96},{40,104},{48,112},{56,120},{... | collective-permute-start | bytes 196616 | tf_op jit(solution)/shard_map/ppermute | solution.py:247
  268.2 9.0 %collective-permute-start.32 = (f32[64,1024]{1,0:T(8,128)S(1)}, f32[64,1024]{1,0:T(8,128)S(1)}, u32[]{:S(2)}, u32[]{:S(2)}) collective-permute-start(f32[64,1024]{1,0:T(8,128)S(1)} %slice_bitcast_fusion), channel_id=1, source_target_pairs={{0,64},{8,72},{16,80},{24,88},{32,96},{40,104},{48,112},{56,120},{... | collective-permute-start | bytes 786440 | tf_op jit(solution)/shard_map/ppermute | solution.py:247
  268.3 1.6 collective-permute-start.27
Sparse Core Ops, SparseCore 0:
  124.4 53.3 reduce-scatter.2
  180.2 52.6 reduce-scatter.4

commit v2 on v1

--- a/solution.py
+++ b/solution.py
@@ -1,6 +1,8 @@
 import functools
+
 import jax
 import jax.numpy as jnp
+import numpy as np
 from jax import lax
 from jax.experimental import pallas as pl
 from jax.experimental.pallas import tpu as pltpu
@@ -131,7 +133,7 @@
 ):
     first = dot3(split(edge_ref[...]), (right_high_ref[...], right_low_ref[...]), NN)
     swap_into(first, first_high, first_low)
-    mixed = dot3(split(site_matrix_ref[...]), (first_high[...], first_low[...]), NN)
+    mixed = dot3(split(site_matrix_ref[...]), (first_high[...], first_low[...]), TN)
     unswap_into(mixed, second_high, second_low)
     site = dot3((first_high[...], first_low[...]), (swapped_high_ref[...], swapped_low_ref[...]), NT)
 
@@ -262,59 +264,65 @@
 
 def on_device(edge_tensor, site_tensor, left_isometry, right_isometry, cotangent):
     row = lax.axis_index("row").astype(jnp.int32)
-    z, y, core = row // 8, row // 2 % 4, row % 2
+    z, y, core = row >> 3, (row >> 1) & 3, row & 1
     edge_rows = edge_tensor.reshape(1024, 1024)
     left_rows = left_isometry.reshape(1024, 1024)
-    back_site = jnp.transpose(site_tensor, (2, 1, 3, 0)).reshape(256, 256)
-    front_site = jnp.transpose(site_tensor, (3, 0, 2, 1)).reshape(256, 256)
 
     def offset_of(other_z, steps, other_core):
-        return ((z ^ other_z) * 8 + (y - steps) % 4 * 2 + (core ^ other_core)) * 64
+        other_z, steps, other_core = (np.array(list(v), np.int32) for v in (other_z, steps, other_core))
+        return ((z ^ other_z) * 8 + ((y - steps) & 3) * 2 + (core ^ other_core)) * 64
 
     own = dense(cotangent)
-    pair = jnp.concatenate([own, row_permute(own, 1, 0, 0)], 0)
-    pieces = [pair] + [row_permute(pair, 0, steps, 0) for steps in (1, 3, 2)]
+    own, right_isometry = lax.optimization_barrier((own, right_isometry))
+    other = row_permute(own, 1, 0, 0)
+    early = own
+    own = dense(right_isometry)
+    others = [row_permute(own, 0, steps, 0) for steps in (1, 3, 2)]
+    quad, other = lax.optimization_barrier((jnp.concatenate([own, *others], 0), other))
+
+    pair = jnp.concatenate([early, other], 0)
+
+    site_matrix = jnp.transpose(site_tensor, (2, 1, 3, 0)).reshape(256, 256)
+    near = [row_permute(pair, 0, steps, 0) for steps in (1, 3)]
+    far = row_permute(pair, 0, 2, 0)
+    quads = [quad, row_permute(quad, 1, 0, 0)]
+    near[0], near[1], site_matrix = lax.optimization_barrier((*near, site_matrix))
+    pieces = [pair, *near, far]
     pieces += [row_permute(piece, 0, 0, 1) for piece in pieces]
-    offsets = jnp.stack([offset_of(j, steps, c) for c in (0, 1) for steps in (0, 1, 3, 2) for j in (0, 1)])
-    cotangent_high, cotangent_low, *rest = back_call(offsets, pieces, left_rows, back_site)
+    order = [(j, steps, c) for c in (0, 1) for steps in (0, 1, 3, 2) for j in (0, 1)]
+    cotangent_high, cotangent_low, *rest = back_call(offset_of(*zip(*order)), pieces, left_rows, site_matrix)
     back_split, swapped_split = rest[:2], rest[2:]
 
-    own = dense(right_isometry)
-    quad = jnp.concatenate([own] + [row_permute(own, 0, steps, 0) for steps in (1, 3, 2)], 0)
-    pieces = [quad, row_permute(quad, 1, 0, 0)]
-    pieces += [row_permute(piece, 0, 0, 1) for piece in pieces]
-    offsets = jnp.stack([offset_of(j, steps, c) for c in (0, 1) for j in (0, 1) for steps in (0, 1, 3, 2)])
-
-    blocks = [(i % 2) * 8 + i // 2 for i in range(16)]
-    places = jnp.stack(
-        [((b % 2 ^ core) * 8 + (b // 2 % 4 - y) % 4 * 2 + (b // 8 ^ z)) * 64 for b in blocks]
-    )
-    right_own, right_other = right_call(places, back_split, edge_rows)
-
-    right_high, right_low, edge_terms = edge_call(offsets, pieces, back_split)
+    quads += [row_permute(piece, 0, 0, 1) for piece in quads]
+    order = [(j, steps, c) for c in (0, 1) for j in (0, 1) for steps in (0, 1, 3, 2)]
+    right_high, right_low, edge_terms = edge_call(offset_of(*zip(*order)), quads, back_split)
     edge_gradient = lax.psum_scatter(edge_terms, "col", scatter_dimension=0, tiled=True)
     left_terms, site_terms = left_call(
-        edge_rows, (right_high, right_low), front_site, swapped_split, (cotangent_high, cotangent_low)
+        edge_rows, (right_high, right_low), site_matrix, swapped_split, (cotangent_high, cotangent_low)
     )
     left_gradient = lax.psum_scatter(left_terms, "col", scatter_dimension=0, tiled=True)
 
-    total = (right_own + row_permute(right_other, 0, 0, 1)).reshape(4, 2, 64, 1024)
-    total = total[0] + row_permute(total[1], 0, 1, 0) + row_permute(total[3], 0, 3, 0) + row_permute(total[2], 0, 2, 0)
-    right_gradient = total[0] + row_permute(total[1], 1, 0, 0)
+    blocks = np.array([(i % 2) * 8 + i // 2 for i in range(16)], np.int32)
+    places = ((blocks & 1) ^ core) * 8 + (((blocks >> 1) - y) & 3) * 2 + ((blocks >> 3) ^ z)
+    right_own, right_other = right_call(places * 64, back_split, edge_rows)
 
     part = site_terms.reshape(2, 128, 256)
     part = (take(part, core) + row_permute(take(part, 1 - core), 0, 0, 1)).reshape(2, 64, 256)
     part = (take(part, z) + row_permute(take(part, 1 - z), 1, 0, 0)).reshape(4, 16, 256)
-    part = take(part, y) + sum(row_permute(take(part, (y + k) % 4), 0, k, 0) for k in (1, 2, 3))
+    part = take(part, y) + sum(row_permute(take(part, (y + k) & 3), 0, k, 0) for k in (1, 2, 3))
     part = part + sum(col_permute(part, 0, k) for k in (1, 2, 3))
     part = part + col_permute(part, 1, 0)
     ring = [part] + [row_permute(part, 0, k, 0) for k in (3, 2, 1)]
-    part = lax.dynamic_slice_in_dim(jnp.concatenate(ring + ring, 0), (4 - y) % 4 * 16, 64, 0)
+    part = lax.dynamic_slice_in_dim(jnp.concatenate(ring + ring, 0), ((4 - y) & 3) * 16, 64, 0)
     other = row_permute(part, 1, 0, 0)
     part = jnp.where(z == 0, jnp.concatenate([part, other], 0), jnp.concatenate([other, part], 0))
     other = row_permute(part, 0, 0, 1)
     part = jnp.where(core == 0, jnp.concatenate([part, other], 0), jnp.concatenate([other, part], 0))
     site_gradient = jnp.transpose(part.reshape(16, 16, 16, 16), (3, 1, 0, 2))
+
+    total = (right_own + row_permute(right_other, 0, 0, 1)).reshape(4, 2, 64, 1024)
+    total = total[0] + row_permute(total[1], 0, 1, 0) + row_permute(total[3], 0, 3, 0) + row_permute(total[2], 0, 2, 0)
+    right_gradient = total[0] + row_permute(total[1], 1, 0, 0)
 
     return (
         jnp.transpose(edge_gradient, (1, 0, 2)),
@@ -333,6 +341,5 @@
         P("col", None, "row"),
     )
     out_specs = (P("row", "col", None), P(), P("row", "col", None), P("col", "row", None))
-    return jax.shard_map(
-        on_device, mesh=mesh, in_specs=in_specs, out_specs=out_specs, check_vma=False
-    )
+
+    return jax.shard_map(on_device, mesh=mesh, in_specs=in_specs, out_specs=out_specs, check_vma=False)

time: 290 us -> 252 us (0.87)
  waiting for transfers between devices: 122 us -> 65.8 us
  starting transfers between devices: 45.5 us -> 74 us
  local copies, waits for them, and re-layouts: 28.9 us -> 18 us
    ppermute x29, starting transfers between devices: 40.9 us -> 69.9 us  [row_permute(): return lax.ppermute(value, 'row', pairs)]
    ppermute x4, waiting for transfers between devices: 34.8 us -> 6.3 us  [col_permute(): lax.ppermute(value, 'col', [(i, (i // 4 ^ z) * 4 + (i + x) % 4) for i in...]
    ppermute x29, waiting for transfers between devices: 86.8 us -> 59.5 us  [row_permute(): return lax.ppermute(value, 'row', pairs)]
    reshape x2 -> x1, local copies, waits for them, and re-layouts: 6.11 us -> 1.54 us  [on_device(): site_matrix = jnp.transpose(site_tensor, (2, 1, 3, 0)).reshape(256, 256)]
    unnamed x25 -> x38, local copies, waits for them, and re-layouts: 10.2 us -> 8.69 us
  transfers between devices with their start and end apart: 35 -> 35, of which waited for: 18 -> 22; matrix products, arithmetic and copies ran while one was open for 9% -> 6% of each run, Pallas kernels for 22% -> 25%
where the time goes in v2:
time: 252 us
  Pallas kernels  76.4 us (30%)
  starting transfers between devices  74 us (29%)
  waiting for transfers between devices  65.8 us (26%)
  local copies, waits for them, and re-layouts  18 us (7%)
  between operations  14.4 us (6%)
  other arithmetic  2.98 us (1%)
    ppermute x29, starting transfers between devices, row_permute(): return lax.ppermute(value, 'row', pairs)  69.9 us
    ppermute x29, waiting for transfers between devices, row_permute(): return lax.ppermute(value, 'row', pairs)  59.5 us
    pallas_call x1, Pallas kernels, left_call(): pl.pallas_call(left_kernel, out_shape=(jax.ShapeDtypeStruct((16, 64, 1024...  31.7 us
    pallas_call x1, Pallas kernels, back_call(): pl.pallas_call(functools.partial(back_kernel, len(pieces)), out_shape=(SQ...  17.2 us
    pallas_call x1, Pallas kernels, edge_call(): pl.pallas_call(functools.partial(edge_kernel, len(pieces)), out_shape=(SQ...  14.2 us
    pallas_call x1, Pallas kernels, right_call(): pl.pallas_call(right_kernel, out_shape=(jax.ShapeDtypeStruct((512, 1024),...  13.2 us
    unnamed x38, local copies, waits for them, and re-layouts  8.69 us
    ppermute x4, waiting for transfers between devices, col_permute(): lax.ppermute(value, 'col', [(i, (i // 4 ^ z) * 4 + (i + x) % 4) for i in...  6.3 us
  transfers between devices with their start and end apart: 35, of which 22 were waited for; matrix products, arithmetic and copies ran while one was open for 6% of the time, Pallas kernels for 25%

profile of v2, /device:TPU:1, one launch (start us, length us, event | category | flops | bytes accessed | tf_op | source)
XLA Modules:
  0.0 251.5 jit_solution(9184981063810950800)
XLA Ops:
  7.2 1.6 copy.23
  8.8 0.5 reshape.56
  9.3 0.5 copy.24
  10.3 3.8 %collective-permute-start.2 = (f32[64,1024]{1,0:T(8,128)S(1)}, f32[64,1024]{1,0:T(8,128)S(1)}, u32[]{:S(2)}, u32[]{:S(2)}) collective-permute-start(f32[64,1024]{1,0:T(8,128)S(1)} %reshape.58), channel_id=1, source_target_pairs={{0,32},{8,40},{16,48},{24,56},{32,0},{40,8},{48,16},{56,24},{64,96... | collective-permute-start | bytes 786440 | tf_op jit(solution)/shard_map/ppermute | solution.py:249
  14.1 0.8 collective-permute-start.1
  14.8 0.7 collective-permute-start
  15.5 3.6 %collective-permute-start.3 = (f32[64,1024]{1,0:T(8,128)S(1)}, f32[64,1024]{1,0:T(8,128)S(1)}, u32[]{:S(2)}, u32[]{:S(2)}) collective-permute-start(f32[64,1024]{1,0:T(8,128)S(1)} %reshape.56), channel_id=1, source_target_pairs={{0,64},{8,72},{16,80},{24,88},{32,96},{40,104},{48,112},{56,120},{... | collective-permute-start | bytes 786440 | tf_op jit(solution)/shard_map/ppermute | solution.py:249
  19.1 0.7 collective-permute-done.2
  19.9 6.0 %collective-permute-done.1 = f32[64,1024]{1,0:T(8,128)S(1)} collective-permute-done((f32[64,1024]{1,0:T(8,128)S(1)}, f32[64,1024]{1,0:T(8,128)S(1)}, u32[]{:S(2)}, u32[]{:S(2)}) %collective-permute-start.1) | collective-permute-done | bytes 262176 | tf_op jit(solution)/shard_map/ppermute | solution.py:249
  26.3 3.7 %collective-permute-start.4 = (f32[256,1024]{1,0:T(8,128)S(1)}, f32[256,1024]{1,0:T(8,128)}, u32[]{:S(2)}, u32[]{:S(2)}) collective-permute-start(f32[256,1024]{1,0:T(8,128)S(1)} %pad_maximum_fusion.refs_0_), channel_id=1, source_target_pairs={{0,64},{8,72},{16,80},{24,88},{32,96},{40,104},{48,112},{56,120},{... | collective-permute-start | bytes 3145736 | tf_op jit(solution)/shard_map/ppermute | solution.py:249
  30.1 0.7 constant_dynamic-update-slice_fusion.1
  30.8 0.7 constant_dynamic-update-slice_fusion.refs_0_
  31.5 1.5 collective-permute-start.7
  33.0 1.4 collective-permute-start.8
  34.5 1.6 collective-permute-start.9
  36.1 1.6 collective-permute-start.10
  37.7 8.0 %collective-permute-done.7.refs_1_ = f32[128,1024]{1,0:T(8,128)S(1)} collective-permute-done((f32[128,1024]{1,0:T(8,128)}, f32[128,1024]{1,0:T(8,128)S(1)}, u32[]{:S(2)}, u32[]{:S(2)}) %collective-permute-start.7) | collective-permute-done | bytes 524320 | tf_op jit(solution)/shard_map/ppermute | solution.py:249
  45.7 1.9 collective-permute-start.5
  47.6 5.0 %collective-permute-done.4.refs_1_ = f32[256,1024]{1,0:T(8,128)} collective-permute-done((f32[256,1024]{1,0:T(8,128)S(1)}, f32[256,1024]{1,0:T(8,128)}, u32[]{:S(2)}, u32[]{:S(2)}) %collective-permute-start.4) | collective-permute-done | bytes 1048608 | tf_op jit(solution)/shard_map/ppermute | solution.py:249
  52.6 1.7 collective-permute-start.6
  54.3 2.2 copy.25
  56.6 1.5 reshape.59.refs_9_.site_matrix_ref
  58.4 1.6 collective-permute-start.12
  60.1 0.6 fusion.4
  60.8 1.1 collective-permute-done.12.refs_6_
  61.8 0.7 collective-permute-done.13.refs_7_
  62.6 0.7 copy-done.4
  63.3 17.2 %back.1 = (bf16[1024,1024]{1,0:T(8,128)(2,1)}, bf16[1024,1024]{1,0:T(8,128)(2,1)}, bf16[1024,1024]{1,0:T(8,128)(2,1)}, bf16[1024,1024]{1,0:T(8,128)(2,1)}, bf16[...) custom-call(s32[16]{0:T(128)} %get-tuple-element.62.offsets_ref, ...), custom_call_target="tpu_custom_call" | custom-call | tf_op jit(solution)/shard_map/back/pallas_call | solution.py:179
  80.6 14.2 %edge.1 = (bf16[1024,1024]{1,0:T(8,128)(2,1)}, bf16[1024,1024]{1,0:T(8,128)(2,1)}, f32[16,64,1024]{2,1,0:T(8,128)}) custom-call(s32[16]{0:T(128)} %get-tuple-element.63.offsets_ref, f32[256,1024]{1,0:T(8,128)} %copy-done, f32[256,1024]{1,0:T(8,128)} %collective-permute-done.4.refs_1_, f32[256,1024]{1,0:T(8,128)} %collective-permute-done.5.refs_2_, ...), custom_call_target="tpu_custom_call" | custom-call | tf_op jit(solution)/shard_map/edge/pallas_call | solution.py:195
  94.9 31.7 %left.1 = (f32[16,64,1024]{2,1,0:T(8,128)}, f32[256,256]{1,0:T(8,128)}) custom-call(f32[1024,1024]{1,0:T(8,128)} %bitcast.41, bf16[1024,1024]{1,0:T(8,128)(2,1)} %get-tuple-element.34.right_high_ref, bf16[1024,1024]{1,0:T(8,128)(2,1)} %get-tuple-element.35.right_low_ref, f32[256,256]{1,0:T(8,128)} %reshape.59.refs_9_.site_matrix_ref, ...), custom_call_target="tpu_custom_call" | custom-call | tf_op jit(solution)/shard_map/left/pallas_call | solution.py:211
  126.7 13.2 %right.1 = (f32[512,1024]{1,0:T(8,128)}, f32[512,1024]{1,0:T(8,128)}) custom-call(s32[16]{0:T(128)} %get-tuple-element.61.places_ref, bf16[1024,1024]{1,0:T(8,128)(2,1)} %get-tuple-element.31.refs_4_.back_high_ref, bf16[1024,1024]{1,0:T(8,128)(2,1)} %get-tuple-element.32.refs_5_.back_low_ref, f32[1024,1024]{1,0:T(8,128)} %bitcast.42), custom_call_target="tpu_custom_call" | custom-call | tf_op jit(solution)/shard_map/right/pallas_call | solution.py:229
  140.7 3.7 %collective-permute-done.14 = f32[128,256]{1,0:T(8,128)S(1)} collective-permute-done((f32[128,256]{1,0:T(8,128)S(1)}, f32[128,256]{1,0:T(8,128)S(1)}, u32[]{:S(2)}, u32[]{:S(2)}) %collective-permute-start.14) | collective-permute-done | bytes 131104 | tf_op jit(solution)/shard_map/ppermute | solution.py:249
  144.4 2.3 collective-permute-start.15
  146.7 5.4 %collective-permute-done.15 = f32[64,256]{1,0:T(8,128)S(1)} collective-permute-done((f32[64,256]{1,0:T(8,128)S(1)}, f32[64,256]{1,0:T(8,128)S(1)}, u32[]{:S(2)}, u32[]{:S(2)}) %collective-permute-start.15) | collective-permute-done | bytes 65568 | tf_op jit(solution)/shard_map/ppermute | solution.py:249
  152.1 2.5 %collective-permute-start.18 = (f32[16,256]{1,0:T(8,128)S(1)}, f32[16,256]{1,0:T(8,128)S(1)}, u32[]{:S(2)}, u32[]{:S(2)}) collective-permute-start(f32[16,256]{1,0:T(8,128)S(1)} %get-tuple-element.59), channel_id=1, source_target_pairs={{0,48},{8,56},{16,0},{24,8},{32,16},{40,24},{48,32},{56,40},{64,11... | collective-permute-start | bytes 49160 | tf_op jit(solution)/shard_map/ppermute | solution.py:249
  154.7 1.8 collective-permute-start.17
  156.5 2.0 collective-permute-done.16
  158.8 1.6 collective-permute-start.21
  160.3 1.7 collective-permute-start.20
  162.1 2.3 collective-permute-done.19
  164.4 0.7 collective-permute-done.20
  165.1 0.7 collective-permute-start.22
  165.7 3.3 %collective-permute-done.22 = f32[16,256]{1,0:T(8,128)S(1)} collective-permute-done((f32[16,256]{1,0:T(8,128)S(1)}, f32[16,256]{1,0:T(8,128)S(1)}, u32[]{:S(2)}, u32[]{:S(2)}) %collective-permute-start.22) | collective-permute-done | bytes 16416 | tf_op jit(solution)/shard_map/ppermute | solution.py:253
  169.1 2.0 collective-permute-start.23
  171.0 1.2 collective-permute-start.24
  172.2 0.8 collective-permute-start.25
  173.0 2.5 %collective-permute-done.24 = f32[16,256]{1,0:T(8,128)S(1)} collective-permute-done((f32[16,256]{1,0:T(8,128)S(1)}, f32[16,256]{1,0:T(8,128)S(1)}, u32[]{:S(2)}, u32[]{:S(2)}) %collective-permute-start.24) | collective-permute-done | bytes 16416 | tf_op jit(solution)/shard_map/ppermute | solution.py:249
  175.5 0.9 collective-permute-done.25
  176.4 2.0 add.132
  178.7 0.6 collective-permute-start.31
  179.3 1.4 collective-permute-start.30
  180.8 2.2 collective-permute-start.26
  183.1 5.7 %collective-permute-done.31 = f32[2,64,1024]{2,1,0:T(8,128)S(1)} collective-permute-done((f32[2,64,1024]{2,1,0:T(8,128)S(1)}, f32[2,64,1024]{2,1,0:T(8,128)S(1)}, u32[]{:S(2)}, u32[]{:S(2)}) %collective-permute-start.31) | collective-permute-done | bytes 524320 | tf_op jit(solution)/shard_map/ppermute | solution.py:249
  188.8 3.7 %collective-permute-done.30 = f32[2,64,1024]{2,1,0:T(8,128)S(1)} collective-permute-done((f32[2,64,1024]{2,1,0:T(8,128)S(1)}, f32[2,64,1024]{2,1,0:T(8,128)S(1)}, u32[]{:S(2)}, u32[]{:S(2)}) %collective-permute-start.30) | collective-permute-done | bytes 524320 | tf_op jit(solution)/shard_map/ppermute | solution.py:249
  192.5 1.9 collective-permute-done.29
  194.5 1.3 collective-permute-start.32
  195.9 10.2 %collective-permute-done.26 = f32[64,256]{1,0:T(8,128)S(1)} collective-permute-done((f32[64,256]{1,0:T(8,128)S(1)}, f32[64,256]{1,0:T(8,128)S(1)}, u32[]{:S(2)}, u32[]{:S(2)}) %collective-permute-start.26) | collective-permute-done | bytes 65568 | tf_op jit(solution)/shard_map/ppermute | solution.py:249
  206.0 28.9 %collective-permute-start.27 = (f32[128,256]{1,0:T(8,128)S(1)}, f32[128,256]{1,0:T(8,128)S(1)}, u32[]{:S(2)}, u32[]{:S(2)}) collective-permute-start(f32[128,256]{1,0:T(8,128)S(1)} %maximum_select_fusion.1), channel_id=1, source_target_pairs={{0,8},{8,0},{16,24},{24,16},{32,40},{40,32},{48,56},{56,48},{64,72... | collective-permute-start | bytes 393224 | tf_op jit(solution)/shard_map/ppermute | solution.py:249
  235.0 1.0 collective-permute-done.27
  236.0 0.6 select_n.63
  236.6 2.6 %copy.27 = f32[16,16,16,16]{3,2,1,0:T(8,128)} copy(f32[16,16,16,16]{0,3,1,2:T(8,128)S(1)} %bitcast.43) | data formatting | bytes 524288
  239.3 0.9 reshape.65
  240.2 2.2 copy.26
  242.4 2.2 copy.28
  (78 shorter events, 3.3 us)
Async XLA Ops:
  7.2 2.1 copy-start.5
  7.2 233.0 %reduce-scatter.3.cloned.1.call-start = ((), (), s32[]{:S(2)}) async-start(), calls=%async_computation.2 | async-start | bytes 4718592 | tf_op jit(solution)/shard_map/reduce_scatter | solution.py:299
  10.3 9.6 %collective-permute-start.2 = (f32[64,1024]{1,0:T(8,128)S(1)}, f32[64,1024]{1,0:T(8,128)S(1)}, u32[]{:S(2)}, u32[]{:S(2)}) collective-permute-start(f32[64,1024]{1,0:T(8,128)S(1)} %reshape.58), channel_id=1, source_target_pairs={{0,32},{8,40},{16,48},{24,56},{32,0},{40,8},{48,16},{56,24},{64,96... | collective-permute-start | bytes 786440 | tf_op jit(solution)/shard_map/ppermute | solution.py:249
  14.1 11.8 %collective-permute-start.1 = (f32[64,1024]{1,0:T(8,128)S(1)}, f32[64,1024]{1,0:T(8,128)S(1)}, u32[]{:S(2)}, u32[]{:S(2)}) collective-permute-start(f32[64,1024]{1,0:T(8,128)S(1)} %reshape.58), channel_id=1, source_target_pairs={{0,48},{8,56},{16,0},{24,8},{32,16},{40,24},{48,32},{56,40},{64,11... | collective-permute-start | bytes 786440 | tf_op jit(solution)/shard_map/ppermute | solution.py:249
  14.8 11.4 %collective-permute-start = (f32[64,1024]{1,0:T(8,128)S(1)}, f32[64,1024]{1,0:T(8,128)S(1)}, u32[]{:S(2)}, u32[]{:S(2)}) collective-permute-start(f32[64,1024]{1,0:T(8,128)S(1)} %reshape.58), channel_id=1, source_target_pairs={{0,16},{8,24},{16,32},{24,40},{32,48},{40,56},{48,0},{56,8},{64,80... | collective-permute-start | bytes 786440 | tf_op jit(solution)/shard_map/ppermute | solution.py:249
  15.5 10.8 %collective-permute-start.3 = (f32[64,1024]{1,0:T(8,128)S(1)}, f32[64,1024]{1,0:T(8,128)S(1)}, u32[]{:S(2)}, u32[]{:S(2)}) collective-permute-start(f32[64,1024]{1,0:T(8,128)S(1)} %reshape.56), channel_id=1, source_target_pairs={{0,64},{8,72},{16,80},{24,88},{32,96},{40,104},{48,112},{56,120},{... | collective-permute-start | bytes 786440 | tf_op jit(solution)/shard_map/ppermute | solution.py:249
  26.3 30.2 %copy-start = (f32[256,1024]{1,0:T(8,128)}, f32[256,1024]{1,0:T(8,128)S(1)}, u32[]{:S(2)}) copy-start(f32[256,1024]{1,0:T(8,128)S(1)} %pad_maximum_fusion.refs_0_) | copy-start | bytes 3145732
  26.3 26.3 %collective-permute-start.4 = (f32[256,1024]{1,0:T(8,128)S(1)}, f32[256,1024]{1,0:T(8,128)}, u32[]{:S(2)}, u32[]{:S(2)}) collective-permute-start(f32[256,1024]{1,0:T(8,128)S(1)} %pad_maximum_fusion.refs_0_), channel_id=1, source_target_pairs={{0,64},{8,72},{16,80},{24,88},{32,96},{40,104},{48,112},{56,120},{... | collective-permute-start | bytes 3145736 | tf_op jit(solution)/shard_map/ppermute | solution.py:249
  31.5 14.2 %collective-permute-start.7 = (f32[128,1024]{1,0:T(8,128)}, f32[128,1024]{1,0:T(8,128)S(1)}, u32[]{:S(2)}, u32[]{:S(2)}) collective-permute-start(f32[128,1024]{1,0:T(8,128)} %constant_dynamic-update-slice_fusion.refs_0_), channel_id=1, source_target_pairs={{0,16},{8,24},{16,32},{24,40},{32,48},{40,56},{48,0},{56,8},{64,80... | collective-permute-start | bytes 1572872 | tf_op jit(solution)/shard_map/ppermute | solution.py:249
  33.0 25.1 %collective-permute-start.8 = (f32[128,1024]{1,0:T(8,128)}, f32[128,1024]{1,0:T(8,128)}, u32[]{:S(2)}, u32[]{:S(2)}) collective-permute-start(f32[128,1024]{1,0:T(8,128)} %constant_dynamic-update-slice_fusion.refs_0_), channel_id=1, source_target_pairs={{0,48},{8,56},{16,0},{24,8},{32,16},{40,24},{48,32},{56,40},{64,11... | collective-permute-start | bytes 1572872 | tf_op jit(solution)/shard_map/ppermute | solution.py:249
  34.5 24.0 %collective-permute-start.9 = (f32[128,1024]{1,0:T(8,128)}, f32[128,1024]{1,0:T(8,128)}, u32[]{:S(2)}, u32[]{:S(2)}) collective-permute-start(f32[128,1024]{1,0:T(8,128)} %constant_dynamic-update-slice_fusion.refs_0_), channel_id=1, source_target_pairs={{0,32},{8,40},{16,48},{24,56},{32,0},{40,8},{48,16},{56,24},{64,96... | collective-permute-start | bytes 1572872 | tf_op jit(solution)/shard_map/ppermute | solution.py:249
  36.1 24.0 %collective-permute-start.10 = (f32[128,1024]{1,0:T(8,128)}, f32[128,1024]{1,0:T(8,128)}, u32[]{:S(2)}, u32[]{:S(2)}) collective-permute-start(f32[128,1024]{1,0:T(8,128)} %constant_dynamic-update-slice_fusion.refs_0_), channel_id=1, source_target_pairs={{0,8},{8,0},{16,24},{24,16},{32,40},{40,32},{48,56},{56,48},{64,72... | collective-permute-start | bytes 1572872 | tf_op jit(solution)/shard_map/ppermute | solution.py:249
  45.7 8.6 %copy-start.1 = (f32[128,1024]{1,0:T(8,128)}, f32[128,1024]{1,0:T(8,128)S(1)}, u32[]{:S(2)}) copy-start(f32[128,1024]{1,0:T(8,128)S(1)} %collective-permute-done.7.refs_1_) | copy-start | bytes 1572868
  45.7 34.9 %collective-permute-start.5 = (f32[256,1024]{1,0:T(8,128)S(1)}, f32[256,1024]{1,0:T(8,128)}, u32[]{:S(2)}, u32[]{:S(2)}) collective-permute-start(f32[256,1024]{1,0:T(8,128)S(1)} %pad_maximum_fusion.refs_0_), channel_id=1, source_target_pairs={{0,8},{8,0},{16,24},{24,16},{32,40},{40,32},{48,56},{56,48},{64,72... | collective-permute-start | bytes 3145736 | tf_op jit(solution)/shard_map/ppermute | solution.py:249
  52.6 28.0 %collective-permute-start.6 = (f32[256,1024]{1,0:T(8,128)}, f32[256,1024]{1,0:T(8,128)}, u32[]{:S(2)}, u32[]{:S(2)}) collective-permute-start(f32[256,1024]{1,0:T(8,128)} %collective-permute-done.4.refs_1_), channel_id=1, source_target_pairs={{0,8},{8,0},{16,24},{24,16},{32,40},{40,32},{48,56},{56,48},{64,72... | collective-permute-start | bytes 3145736 | tf_op jit(solution)/shard_map/ppermute | solution.py:249
  56.5 3.6 %copy-start.7 = (s32[16]{0:T(128)S(1)}, s32[16]{0:T(128)}, u32[]{:S(2)}) copy-start(s32[16]{0:T(128)} %constant.64.clone) | copy-start | bytes 196
  56.5 3.5 %copy-start.8 = (s32[16]{0:T(128)S(1)}, s32[16]{0:T(128)}, u32[]{:S(2)}) copy-start(s32[16]{0:T(128)} %constant.70.clone) | copy-start | bytes 196
  56.5 3.5 %copy-start.9 = (s32[16]{0:T(128)S(1)}, s32[16]{0:T(128)}, u32[]{:S(2)}) copy-start(s32[16]{0:T(128)} %constant.69.clone) | copy-start | bytes 196
  56.6 3.5 %copy-start.10 = (s32[16]{0:T(128)S(1)}, s32[16]{0:T(128)}, u32[]{:S(2)}) copy-start(s32[16]{0:T(128)} %constant.66.clone) | copy-start | bytes 196
  56.6 3.5 %copy-start.11 = (s32[16]{0:T(128)S(1)}, s32[16]{0:T(128)}, u32[]{:S(2)}) copy-start(s32[16]{0:T(128)} %constant.72) | copy-start | bytes 196
  56.6 3.5 %copy-start.12 = (s32[16]{0:T(128)S(1)}, s32[16]{0:T(128)}, u32[]{:S(2)}) copy-start(s32[16]{0:T(128)} %constant.71) | copy-start | bytes 196
  56.6 3.5 %copy-start.13 = (s32[16]{0:T(128)S(1)}, s32[16]{0:T(128)}, u32[]{:S(2)}) copy-start(s32[16]{0:T(128)} %constant.67.clone) | copy-start | bytes 196
  58.1 2.6 %collective-permute-start.11 = (f32[128,1024]{1,0:T(8,128)}, f32[128,1024]{1,0:T(8,128)S(1)}, u32[]{:S(2)}, u32[]{:S(2)}) collective-permute-start(f32[128,1024]{1,0:T(8,128)} %copy-done.1), channel_id=1, source_target_pairs={{0,8},{8,0},{16,24},{24,16},{32,40},{40,32},{48,56},{56,48},{64,72... | collective-permute-start | bytes 1572872 | tf_op jit(solution)/shard_map/ppermute | solution.py:249
  58.4 3.4 %collective-permute-start.12 = (f32[128,1024]{1,0:T(8,128)}, f32[128,1024]{1,0:T(8,128)S(1)}, u32[]{:S(2)}, u32[]{:S(2)}) collective-permute-start(f32[128,1024]{1,0:T(8,128)} %collective-permute-done.8.refs_2_), channel_id=1, source_target_pairs={{0,8},{8,0},{16,24},{24,16},{32,40},{40,32},{48,56},{56,48},{64,72... | collective-permute-start | bytes 1572872 | tf_op jit(solution)/shard_map/ppermute | solution.py:249
  60.1 2.5 collective-permute-start.13
  60.8 1.8 copy-start.2
  61.8 0.8 copy-start.3
  62.6 0.8 copy-start.4
  94.9 147.6 %reduce-scatter.5.cloned.1.call-start = ((), (), s32[]{:S(2)}) async-start(), calls=%async_computation.3 | async-start | bytes 4718592 | tf_op jit(solution)/shard_map/reduce_scatter | solution.py:303
  126.6 13.6 %copy-start.6 = (f32[256,256]{1,0:T(8,128)S(1)}, f32[256,256]{1,0:T(8,128)}, u32[]{:S(2)}) copy-start(f32[256,256]{1,0:T(8,128)} %get-tuple-element.40) | copy-start | bytes 786436
  139.8 36.6 %collective-permute-start.28 = (f32[512,1024]{1,0:T(8,128)}, f32[512,1024]{1,0:T(8,128)S(1)}, u32[]{:S(2)}, u32[]{:S(2)}) collective-permute-start(f32[512,1024]{1,0:T(8,128)} %get-tuple-element.43), channel_id=1, source_target_pairs={{0,8},{8,0},{16,24},{24,16},{32,40},{40,32},{48,56},{56,48},{64,72... | collective-permute-start | bytes 6291464 | tf_op jit(solution)/shard_map/ppermute | solution.py:249
  140.2 4.2 %collective-permute-start.14 = (f32[128,256]{1,0:T(8,128)S(1)}, f32[128,256]{1,0:T(8,128)S(1)}, u32[]{:S(2)}, u32[]{:S(2)}) collective-permute-start(f32[128,256]{1,0:T(8,128)S(1)} %dynamic-slice_bitcast_fusion), channel_id=1, source_target_pairs={{0,8},{8,0},{16,24},{24,16},{32,40},{40,32},{48,56},{56,48},{64,72... | collective-permute-start | bytes 393224 | tf_op jit(solution)/shard_map/ppermute | solution.py:249
  144.4 7.6 %collective-permute-start.15 = (f32[64,256]{1,0:T(8,128)S(1)}, f32[64,256]{1,0:T(8,128)S(1)}, u32[]{:S(2)}, u32[]{:S(2)}) collective-permute-start(f32[64,256]{1,0:T(8,128)S(1)} %dynamic-slice_bitcast_fusion.1), channel_id=1, source_target_pairs={{0,64},{8,72},{16,80},{24,88},{32,96},{40,104},{48,112},{56,120},{... | collective-permute-start | bytes 196616 | tf_op jit(solution)/shard_map/ppermute | solution.py:249
  152.1 4.4 %collective-permute-start.18 = (f32[16,256]{1,0:T(8,128)S(1)}, f32[16,256]{1,0:T(8,128)S(1)}, u32[]{:S(2)}, u32[]{:S(2)}) collective-permute-start(f32[16,256]{1,0:T(8,128)S(1)} %get-tuple-element.59), channel_id=1, source_target_pairs={{0,48},{8,56},{16,0},{24,8},{32,16},{40,24},{48,32},{56,40},{64,11... | collective-permute-start | bytes 49160 | tf_op jit(solution)/shard_map/ppermute | solution.py:249
  154.7 3.8 %collective-permute-start.16 = (f32[16,256]{1,0:T(8,128)S(1)}, f32[16,256]{1,0:T(8,128)S(1)}, u32[]{:S(2)}, u32[]{:S(2)}) collective-permute-start(f32[16,256]{1,0:T(8,128)S(1)} %get-tuple-element.60), channel_id=1, source_target_pairs={{0,16},{8,24},{16,32},{24,40},{32,48},{40,56},{48,0},{56,8},{64,80... | collective-permute-start | bytes 49160 | tf_op jit(solution)/shard_map/ppermute | solution.py:249
  154.7 4.1 %collective-permute-start.17 = (f32[16,256]{1,0:T(8,128)S(1)}, f32[16,256]{1,0:T(8,128)S(1)}, u32[]{:S(2)}, u32[]{:S(2)}) collective-permute-start(f32[16,256]{1,0:T(8,128)S(1)} %get-tuple-element.58), channel_id=1, source_target_pairs={{0,32},{8,40},{16,48},{24,56},{32,0},{40,8},{48,16},{56,24},{64,96... | collective-permute-start | bytes 49160 | tf_op jit(solution)/shard_map/ppermute | solution.py:249
  158.8 3.3 %collective-permute-start.21 = (f32[16,256]{1,0:T(8,128)S(1)}, f32[16,256]{1,0:T(8,128)S(1)}, u32[]{:S(2)}, u32[]{:S(2)}) collective-permute-start(f32[16,256]{1,0:T(8,128)S(1)} %bitcast_add_fusion.2), channel_id=1, source_target_pairs={{0,3},{1,0},{2,1},{3,2},{4,7},{5,4},{6,5},{7,6},{8,11},{9,8},{10,9... | collective-permute-start | bytes 49160 | tf_op jit(solution)/shard_map/ppermute | solution.py:253
  160.3 4.0 %collective-permute-start.19 = (f32[16,256]{1,0:T(8,128)S(1)}, f32[16,256]{1,0:T(8,128)S(1)}, u32[]{:S(2)}, u32[]{:S(2)}) collective-permute-start(f32[16,256]{1,0:T(8,128)S(1)} %bitcast_add_fusion.2), channel_id=1, source_target_pairs={{0,1},{1,2},{2,3},{3,0},{4,5},{5,6},{6,7},{7,4},{8,9},{9,10},{10,1... | collective-permute-start | bytes 49160 | tf_op jit(solution)/shard_map/ppermute | solution.py:253
  160.3 4.7 %collective-permute-start.20 = (f32[16,256]{1,0:T(8,128)S(1)}, f32[16,256]{1,0:T(8,128)S(1)}, u32[]{:S(2)}, u32[]{:S(2)}) collective-permute-start(f32[16,256]{1,0:T(8,128)S(1)} %bitcast_add_fusion.2), channel_id=1, source_target_pairs={{0,2},{1,3},{2,0},{3,1},{4,6},{5,7},{6,4},{7,5},{8,10},{9,11},{10,... | collective-permute-start | bytes 49160 | tf_op jit(solution)/shard_map/ppermute | solution.py:253
  165.1 4.0 %collective-permute-start.22 = (f32[16,256]{1,0:T(8,128)S(1)}, f32[16,256]{1,0:T(8,128)S(1)}, u32[]{:S(2)}, u32[]{:S(2)}) collective-permute-start(f32[16,256]{1,0:T(8,128)S(1)} %add_add_fusion.1), channel_id=1, source_target_pairs={{0,4},{1,5},{2,6},{3,7},{4,0},{5,1},{6,2},{7,3},{8,12},{9,13},{10,... | collective-permute-start | bytes 49160 | tf_op jit(solution)/shard_map/ppermute | solution.py:253
  169.1 3.9 %collective-permute-start.23 = (f32[16,256]{1,0:T(8,128)S(1)}, f32[16,256]{1,0:T(8,128)S(1)}, u32[]{:S(2)}, u32[]{:S(2)}) collective-permute-start(f32[16,256]{1,0:T(8,128)S(1)} %get-tuple-element.53), channel_id=1, source_target_pairs={{0,48},{8,56},{16,0},{24,8},{32,16},{40,24},{48,32},{56,40},{64,11... | collective-permute-start | bytes 49160 | tf_op jit(solution)/shard_map/ppermute | solution.py:249
  171.0 4.5 %collective-permute-start.24 = (f32[16,256]{1,0:T(8,128)S(1)}, f32[16,256]{1,0:T(8,128)S(1)}, u32[]{:S(2)}, u32[]{:S(2)}) collective-permute-start(f32[16,256]{1,0:T(8,128)S(1)} %get-tuple-element.53), channel_id=1, source_target_pairs={{0,32},{8,40},{16,48},{24,56},{32,0},{40,8},{48,16},{56,24},{64,96... | collective-permute-start | bytes 49160 | tf_op jit(solution)/shard_map/ppermute | solution.py:249
  172.2 4.2 %collective-permute-start.25 = (f32[16,256]{1,0:T(8,128)S(1)}, f32[16,256]{1,0:T(8,128)S(1)}, u32[]{:S(2)}, u32[]{:S(2)}) collective-permute-start(f32[16,256]{1,0:T(8,128)S(1)} %get-tuple-element.53), channel_id=1, source_target_pairs={{0,16},{8,24},{16,32},{24,40},{32,48},{40,56},{48,0},{56,8},{64,80... | collective-permute-start | bytes 49160 | tf_op jit(solution)/shard_map/ppermute | solution.py:249
  178.7 10.1 %collective-permute-start.31 = (f32[2,64,1024]{2,1,0:T(8,128)S(1)}, f32[2,64,1024]{2,1,0:T(8,128)S(1)}, u32[]{:S(2)}, u32[]{:S(2)}) collective-permute-start(f32[2,64,1024]{2,1,0:T(8,128)S(1)} %bitcast.57), channel_id=1, source_target_pairs={{0,32},{8,40},{16,48},{24,56},{32,0},{40,8},{48,16},{56,24},{64,96... | collective-permute-start | bytes 1572872 | tf_op jit(solution)/shard_map/ppermute | solution.py:249
  179.3 13.2 %collective-permute-start.30 = (f32[2,64,1024]{2,1,0:T(8,128)S(1)}, f32[2,64,1024]{2,1,0:T(8,128)S(1)}, u32[]{:S(2)}, u32[]{:S(2)}) collective-permute-start(f32[2,64,1024]{2,1,0:T(8,128)S(1)} %bitcast.56), channel_id=1, source_target_pairs={{0,48},{8,56},{16,0},{24,8},{32,16},{40,24},{48,32},{56,40},{64,11... | collective-permute-start | bytes 1572872 | tf_op jit(solution)/shard_map/ppermute | solution.py:249
  180.7 13.6 %collective-permute-start.29 = (f32[2,64,1024]{2,1,0:T(8,128)S(1)}, f32[2,64,1024]{2,1,0:T(8,128)S(1)}, u32[]{:S(2)}, u32[]{:S(2)}) collective-permute-start(f32[2,64,1024]{2,1,0:T(8,128)S(1)} %bitcast.55), channel_id=1, source_target_pairs={{0,16},{8,24},{16,32},{24,40},{32,48},{40,56},{48,0},{56,8},{64,80... | collective-permute-start | bytes 1572872 | tf_op jit(solution)/shard_map/ppermute | solution.py:249
  180.8 25.2 %collective-permute-start.26 = (f32[64,256]{1,0:T(8,128)S(1)}, f32[64,256]{1,0:T(8,128)S(1)}, u32[]{:S(2)}, u32[]{:S(2)}) collective-permute-start(f32[64,256]{1,0:T(8,128)S(1)} %constant_dynamic-slice_fusion), channel_id=1, source_target_pairs={{0,64},{8,72},{16,80},{24,88},{32,96},{40,104},{48,112},{56,120},{... | collective-permute-start | bytes 196616 | tf_op jit(solution)/shard_map/ppermute | solution.py:249
  194.5 44.7 %collective-permute-start.32 = (f32[64,1024]{1,0:T(8,128)S(1)}, f32[64,1024]{1,0:T(8,128)S(1)}, u32[]{:S(2)}, u32[]{:S(2)}) collective-permute-start(f32[64,1024]{1,0:T(8,128)S(1)} %slice_bitcast_fusion), channel_id=1, source_target_pairs={{0,64},{8,72},{16,80},{24,88},{32,96},{40,104},{48,112},{56,120},{... | collective-permute-start | bytes 786440 | tf_op jit(solution)/shard_map/ppermute | solution.py:249
  206.0 29.9 %collective-permute-start.27 = (f32[128,256]{1,0:T(8,128)S(1)}, f32[128,256]{1,0:T(8,128)S(1)}, u32[]{:S(2)}, u32[]{:S(2)}) collective-permute-start(f32[128,256]{1,0:T(8,128)S(1)} %maximum_select_fusion.1), channel_id=1, source_target_pairs={{0,8},{8,0},{16,24},{24,16},{32,40},{40,32},{48,56},{56,48},{64,72... | collective-permute-start | bytes 393224 | tf_op jit(solution)/shard_map/ppermute | solution.py:249
Sparse Core Ops, SparseCore 0:
  95.0 54.9 reduce-scatter.2
  152.4 52.5 reduce-scatter.4

commit v3 on v2

--- a/solution.py
+++ b/solution.py
@@ -64,26 +64,17 @@
     count = 0
     for piece in piece_refs:
         for part in range(piece.shape[0] // block):
-            start = pl.multiple_of(offsets_ref[count], block)
-            copies.append(
-                pltpu.make_async_copy(
-                    piece.at[pl.ds(part * block, block)], whole_ref.at[pl.ds(start, block)], sems.at[count]
-                )
-            )
+            rows = pl.ds(pl.multiple_of(offsets_ref[count], block), block)
+            copy = pltpu.make_async_copy(piece.at[pl.ds(part * block, block)], whole_ref.at[rows], sems.at[count])
+            copies.append((copy, rows))
             count += 1
-    for copy in copies:
+    for copy, _ in copies:
         copy.start()
-    for copy in copies:
+    for copy, rows in copies:
         copy.wait()
-
-    def one(index, carry):
-        rows = pl.ds(pl.multiple_of(index * 64, 64), 64)
         high, low = split(whole_ref[rows, :])
         high_ref[rows, :] = high
         low_ref[rows, :] = low
-        return carry
-
-    lax.fori_loop(0, 16, one, 0)
 
 
 def back_kernel(pieces, offsets_ref, *refs):
@@ -101,21 +92,31 @@
     unswap_into(mixed, back_high, back_low)
 
 
-def edge_kernel(pieces, offsets_ref, *refs):
+def place(terms, sources_ref, staged, ahead_ref, behind_ref, kept_ref):
+    for a in range(16):
+        staged[:, a, :] = terms[16 * a : 16 * a + 16, :]
+    slot = 0
+    for ref in (ahead_ref, behind_ref, kept_ref):
+        for block in range(ref.shape[0]):
+            ref[block] = staged[pl.ds(sources_ref[slot] * 2, 2)]
+            slot += 1
+
+
+def edge_kernel(pieces, offsets_ref, sources_ref, *refs):
     piece_refs = refs[:pieces]
     back_high_ref, back_low_ref = refs[pieces : pieces + 2]
-    whole_high, whole_low, edge_ref, whole, sems = refs[pieces + 2 :]
+    whole_high, whole_low, ahead_ref, behind_ref, kept_ref, whole, staged, sems = refs[pieces + 2 :]
 
     @pl.when(pl.program_id(0) == 0)
     def _():
         assemble(offsets_ref, piece_refs, whole, sems, whole_high, whole_low)
 
     terms = dot3((back_high_ref[...], back_low_ref[...]), (whole_high[...], whole_low[...]), NT)
-    for a in range(16):
-        edge_ref[:, a, :] = terms[16 * a : 16 * a + 16, :]
+    place(terms, sources_ref, staged, ahead_ref, behind_ref, kept_ref)
 
 
 def left_kernel(
+    sources_ref,
     edge_ref,
     right_high_ref,
     right_low_ref,
@@ -124,30 +125,48 @@
     swapped_low_ref,
     cotangent_high_ref,
     cotangent_low_ref,
-    left_ref,
+    ahead_ref,
+    behind_ref,
+    kept_ref,
     site_ref,
     first_high,
     first_low,
     second_high,
     second_low,
+    cotangent_high,
+    cotangent_low,
+    staged,
+    sems,
 ):
+    step = pl.program_id(0)
+    copies = [
+        pltpu.make_async_copy(cotangent_high_ref, cotangent_high, sems.at[0]),
+        pltpu.make_async_copy(cotangent_low_ref, cotangent_low, sems.at[1]),
+    ]
+
+    @pl.when(step == 0)
+    def _():
+        for copy in copies:
+            copy.start()
+
     first = dot3(split(edge_ref[...]), (right_high_ref[...], right_low_ref[...]), NN)
     swap_into(first, first_high, first_low)
     mixed = dot3(split(site_matrix_ref[...]), (first_high[...], first_low[...]), TN)
     unswap_into(mixed, second_high, second_low)
     site = dot3((first_high[...], first_low[...]), (swapped_high_ref[...], swapped_low_ref[...]), NT)
 
-    @pl.when(pl.program_id(0) == 0)
+    @pl.when(step == 0)
     def _():
         site_ref[...] = site
-
-    @pl.when(pl.program_id(0) > 0)
+        for copy in copies:
+            copy.wait()
+
+    @pl.when(step > 0)
     def _():
         site_ref[...] += site
 
-    terms = dot3((second_high[...], second_low[...]), (cotangent_high_ref[...], cotangent_low_ref[...]), NT)
-    for a in range(16):
-        left_ref[:, a, :] = terms[16 * a : 16 * a + 16, :]
+    terms = dot3((second_high[...], second_low[...]), (cotangent_high[...], cotangent_low[...]), NT)
+    place(terms, sources_ref, staged, ahead_ref, behind_ref, kept_ref)
 
 
 def right_kernel(places_ref, back_high_ref, back_low_ref, edge_ref, own_ref, other_ref, turned_high, turned_low, placed):
@@ -191,37 +210,50 @@
     )(offsets, *pieces, rows, site_matrix)
 
 
-def edge_call(offsets, pieces, back_split):
+BLOCKS = tuple(jax.ShapeDtypeStruct((count, 2, 64, 1024), F32) for count in (2, 2, 4))
+BLOCK_SPECS = [pl.BlockSpec((count, 2, 16, 1024), lambda i, *_: (0, 0, i, 0)) for count in (2, 2, 4)]
+
+
+def edge_call(offsets, sources, pieces, back_split):
     return pl.pallas_call(
         functools.partial(edge_kernel, len(pieces)),
-        out_shape=(SQUARE, SQUARE, jax.ShapeDtypeStruct((16, 64, 1024), F32)),
+        out_shape=(SQUARE, SQUARE, *BLOCKS),
+        grid_spec=pltpu.PrefetchScalarGridSpec(
+            num_scalar_prefetch=2,
+            grid=(CHUNKS,),
+            in_specs=[ANY] * len(pieces) + [CHUNK, CHUNK],
+            out_specs=[resident((1024, 1024))] * 2 + BLOCK_SPECS,
+            scratch_shapes=[
+                pltpu.VMEM((1024, 1024), F32),
+                pltpu.VMEM((16, 16, 1024), F32),
+                pltpu.SemaphoreType.DMA((16,)),
+            ],
+        ),
+        compiler_params=PARAMS,
+        name="edge",
+    )(offsets, sources, *pieces, *back_split)
+
+
+def left_call(sources, edge_rows, right_split, site_matrix, swapped_split, cotangent_split):
+    return pl.pallas_call(
+        left_kernel,
+        out_shape=(*BLOCKS, jax.ShapeDtypeStruct((256, 256), F32)),
         grid_spec=pltpu.PrefetchScalarGridSpec(
             num_scalar_prefetch=1,
             grid=(CHUNKS,),
-            in_specs=[ANY] * len(pieces) + [CHUNK, CHUNK],
-            out_specs=[resident((1024, 1024))] * 2 + [pl.BlockSpec((16, 16, 1024), lambda i, *_: (0, i, 0))],
-            scratch_shapes=[pltpu.VMEM((1024, 1024), F32), pltpu.SemaphoreType.DMA((16,))],
+            in_specs=[CHUNK]
+            + [resident((1024, 1024))] * 2
+            + [resident((256, 256))]
+            + [CHUNK] * 2
+            + [ANY] * 2,
+            out_specs=BLOCK_SPECS + [resident((256, 256))],
+            scratch_shapes=[pltpu.VMEM((ROWS, 1024), BF16)] * 4
+            + [pltpu.VMEM((1024, 1024), BF16)] * 2
+            + [pltpu.VMEM((16, 16, 1024), F32), pltpu.SemaphoreType.DMA((2,))],
         ),
         compiler_params=PARAMS,
-        name="edge",
-    )(offsets, *pieces, *back_split)
-
-
-def left_call(edge_rows, right_split, site_matrix, swapped_split, cotangent_split):
-    return pl.pallas_call(
-        left_kernel,
-        out_shape=(jax.ShapeDtypeStruct((16, 64, 1024), F32), jax.ShapeDtypeStruct((256, 256), F32)),
-        grid=(CHUNKS,),
-        in_specs=[CHUNK]
-        + [resident((1024, 1024))] * 2
-        + [resident((256, 256))]
-        + [CHUNK] * 2
-        + [resident((1024, 1024))] * 2,
-        out_specs=[pl.BlockSpec((16, 16, 1024), lambda i: (0, i, 0)), resident((256, 256))],
-        scratch_shapes=[pltpu.VMEM((ROWS, 1024), BF16)] * 4,
-        compiler_params=PARAMS,
         name="left",
-    )(edge_rows, *right_split, site_matrix, *swapped_split, *cotangent_split)
+    )(sources, edge_rows, *right_split, site_matrix, *swapped_split, *cotangent_split)
 
 
 def right_call(places, back_split, edge_rows):
@@ -253,6 +285,16 @@
     return lax.ppermute(value, "col", [(i, ((i // 4) ^ z) * 4 + (i + x) % 4) for i in range(8)])
 
 
+def col_reduce(ahead, behind, kept):
+    from_behind = col_permute(ahead, 0, 1)
+    from_ahead = col_permute(behind, 0, 3)
+    far_behind = col_permute(kept[0] + from_behind[0], 0, 1)
+    far_ahead = col_permute(kept[1] + from_ahead[0], 0, 3)
+    other = kept[3] + from_behind[1] + far_ahead
+    same = kept[2] + from_ahead[1] + far_behind
+    return jnp.transpose(same + col_permute(other, 1, 0), (1, 0, 2))
+
+
 def dense(value):
     cols, bond, width = value.shape
     return jnp.transpose(value.reshape(cols, 2, 8, width), (3, 2, 1, 0)).reshape(width, bond * cols)
@@ -264,6 +306,7 @@
 
 def on_device(edge_tensor, site_tensor, left_isometry, right_isometry, cotangent):
     row = lax.axis_index("row").astype(jnp.int32)
+    col = lax.axis_index("col").astype(jnp.int32)
     z, y, core = row >> 3, (row >> 1) & 3, row & 1
     edge_rows = edge_tensor.reshape(1024, 1024)
     left_rows = left_isometry.reshape(1024, 1024)
@@ -272,14 +315,12 @@
         other_z, steps, other_core = (np.array(list(v), np.int32) for v in (other_z, steps, other_core))
         return ((z ^ other_z) * 8 + ((y - steps) & 3) * 2 + (core ^ other_core)) * 64
 
-    own = dense(cotangent)
-    own, right_isometry = lax.optimization_barrier((own, right_isometry))
-    other = row_permute(own, 1, 0, 0)
-    early = own
+    early = dense(cotangent)
+    early, right_isometry = lax.optimization_barrier((early, right_isometry))
+    other = row_permute(early, 1, 0, 0)
     own = dense(right_isometry)
     others = [row_permute(own, 0, steps, 0) for steps in (1, 3, 2)]
-    quad, other = lax.optimization_barrier((jnp.concatenate([own, *others], 0), other))
-
+    quad = jnp.concatenate([own, *others], 0)
     pair = jnp.concatenate([early, other], 0)
 
     site_matrix = jnp.transpose(site_tensor, (2, 1, 3, 0)).reshape(256, 256)
@@ -295,20 +336,25 @@
 
     quads += [row_permute(piece, 0, 0, 1) for piece in quads]
     order = [(j, steps, c) for c in (0, 1) for j in (0, 1) for steps in (0, 1, 3, 2)]
-    right_high, right_low, edge_terms = edge_call(offset_of(*zip(*order)), quads, back_split)
-    edge_gradient = lax.psum_scatter(edge_terms, "col", scatter_dimension=0, tiled=True)
-    left_terms, site_terms = left_call(
-        edge_rows, (right_high, right_low), site_matrix, swapped_split, (cotangent_high, cotangent_low)
+    steps = np.array([2, 1, 2, 3, 1, 3, 0, 0], np.int32)
+    others = np.array([0, 1, 1, 0, 0, 1, 0, 1], np.int32)
+    sources = ((col >> 2) ^ others) * 4 + ((col + steps) & 3)
+    right_high, right_low, *edge_terms = edge_call(offset_of(*zip(*order)), sources, quads, back_split)
+    edge_gradient = col_reduce(*edge_terms)
+    *left_terms, site_terms = left_call(
+        sources, edge_rows, (right_high, right_low), site_matrix, swapped_split, (cotangent_high, cotangent_low)
     )
-    left_gradient = lax.psum_scatter(left_terms, "col", scatter_dimension=0, tiled=True)
+    left_gradient = col_reduce(*left_terms)
 
     blocks = np.array([(i % 2) * 8 + i // 2 for i in range(16)], np.int32)
     places = ((blocks & 1) ^ core) * 8 + (((blocks >> 1) - y) & 3) * 2 + ((blocks >> 3) ^ z)
     right_own, right_other = right_call(places * 64, back_split, edge_rows)
 
     part = site_terms.reshape(2, 128, 256)
-    part = (take(part, core) + row_permute(take(part, 1 - core), 0, 0, 1)).reshape(2, 64, 256)
-    part = (take(part, z) + row_permute(take(part, 1 - z), 1, 0, 0)).reshape(4, 16, 256)
+    other = row_permute(take(part, 1 - core), 0, 0, 1)
+    part = (take(part, core) + other).reshape(2, 64, 256)
+    other = row_permute(take(part, 1 - z), 1, 0, 0)
+    part = (take(part, z) + other).reshape(4, 16, 256)
     part = take(part, y) + sum(row_permute(take(part, (y + k) & 3), 0, k, 0) for k in (1, 2, 3))
     part = part + sum(col_permute(part, 0, k) for k in (1, 2, 3))
     part = part + col_permute(part, 1, 0)
@@ -321,13 +367,13 @@
     site_gradient = jnp.transpose(part.reshape(16, 16, 16, 16), (3, 1, 0, 2))
 
     total = (right_own + row_permute(right_other, 0, 0, 1)).reshape(4, 2, 64, 1024)
-    total = total[0] + row_permute(total[1], 0, 1, 0) + row_permute(total[3], 0, 3, 0) + row_permute(total[2], 0, 2, 0)
+    total = total[0] + sum(row_permute(total[k], 0, k, 0) for k in (1, 3, 2))
     right_gradient = total[0] + row_permute(total[1], 1, 0, 0)
 
     return (
-        jnp.transpose(edge_gradient, (1, 0, 2)),
+        edge_gradient,
         site_gradient,
-        jnp.transpose(left_gradient, (1, 0, 2)),
+        left_gradient,
         right_gradient.reshape(64, 1, 1024),
     )
 

time: 252 us -> 286 us (1.13)
  waiting for transfers between devices: 65.8 us -> 112 us
  between operations: 14.4 us -> 1.07 us
  other arithmetic: 2.98 us -> 10.9 us
  starting transfers between devices: 74 us -> 69 us
    ppermute x4 -> x14, waiting for transfers between devices: 6.3 us -> 41.1 us  [col_permute(): lax.ppermute(value, 'col', [(i, (i // 4 ^ z) * 4 + (i + x) % 4) for i in...]
    ppermute x29, starting transfers between devices: 69.9 us -> 51.6 us  [row_permute(): return lax.ppermute(value, 'row', pairs)]
    ppermute x4 -> x14, starting transfers between devices: 3.98 us -> 17.5 us  [col_permute(): lax.ppermute(value, 'col', [(i, (i // 4 ^ z) * 4 + (i + x) % 4) for i in...]
    ppermute x29, waiting for transfers between devices: 59.5 us -> 71 us  [row_permute(): return lax.ppermute(value, 'row', pairs)]
    add x3 -> x8, other arithmetic: 0.2 us -> 6.9 us  [the longest x2 2.87 us: col_reduce(): far_behind = col_permute(kept[0] + from_behind[0], 0, 1)]
    unnamed x38 -> x49, local copies, waits for them, and re-layouts: 8.69 us -> 6.73 us
  transfers between devices with their start and end apart: 35 -> 43, of which waited for: 22 -> 23; matrix products, arithmetic and copies ran while one was open for 6% -> 7% of each run, Pallas kernels for 25% -> 10%
where the time goes in v3:
time: 286 us; the launch traced here: 285 us
  waiting for transfers between devices  112 us (39%)
  Pallas kernels  74.8 us (26%)
  starting transfers between devices  69 us (24%)
  local copies, waits for them, and re-layouts  17 us (6%)
  other arithmetic  10.9 us (4%)
    ppermute x29, waiting for transfers between devices, row_permute(): return lax.ppermute(value, 'row', pairs)  71 us
    ppermute x29, starting transfers between devices, row_permute(): return lax.ppermute(value, 'row', pairs)  51.6 us
    ppermute x14, waiting for transfers between devices, col_permute(): lax.ppermute(value, 'col', [(i, (i // 4 ^ z) * 4 + (i + x) % 4) for i in...  41.1 us
    pallas_call x1, Pallas kernels, left_call(): pl.pallas_call(left_kernel, out_shape=(*BLOCKS, jax.ShapeDtypeStruct((256...  31.5 us
    ppermute x14, starting transfers between devices, col_permute(): lax.ppermute(value, 'col', [(i, (i // 4 ^ z) * 4 + (i + x) % 4) for i in...  17.5 us
    pallas_call x1, Pallas kernels, back_call(): pl.pallas_call(functools.partial(back_kernel, len(pieces)), out_shape=(SQ...  16.3 us
    pallas_call x1, Pallas kernels, edge_call(): pl.pallas_call(functools.partial(edge_kernel, len(pieces)), out_shape=(SQ...  13.9 us
    pallas_call x1, Pallas kernels, right_call(): pl.pallas_call(right_kernel, out_shape=(jax.ShapeDtypeStruct((512, 1024),...  13 us
  transfers between devices with their start and end apart: 43, of which 23 were waited for; matrix products, arithmetic and copies ran while one was open for 7% of the time, Pallas kernels for 10%

profile of v3, /device:TPU:1, one launch (start us, length us, event | category | flops | bytes accessed | tf_op | source)
XLA Modules:
  0.0 285.0 jit_solution(705886282763727540)
XLA Ops:
  0.6 1.6 copy.25
  3.7 2.2 collective-permute-start
  5.9 1.5 collective-permute-start.1
  7.4 1.6 collective-permute-start.2
  9.0 4.2 %collective-permute-done = f32[64,1024]{1,0:T(8,128)S(1)} collective-permute-done((f32[64,1024]{1,0:T(8,128)S(1)}, f32[64,1024]{1,0:T(8,128)S(1)}, u32[]{:S(2)}, u32[]{:S(2)}) %collective-permute-start) | collective-permute-done | bytes 262176 | tf_op jit(solution)/shard_map/ppermute | solution.py:281
  13.3 6.6 %collective-permute-done.2 = f32[64,1024]{1,0:T(8,128)S(1)} collective-permute-done((f32[64,1024]{1,0:T(8,128)S(1)}, f32[64,1024]{1,0:T(8,128)S(1)}, u32[]{:S(2)}, u32[]{:S(2)}) %collective-permute-start.2) | collective-permute-done | bytes 262176 | tf_op jit(solution)/shard_map/ppermute | solution.py:281
  19.9 3.7 %collective-permute-start.3 = (f32[256,1024]{1,0:T(8,128)S(1)}, f32[256,1024]{1,0:T(8,128)}, u32[]{:S(2)}, u32[]{:S(2)}) collective-permute-start(f32[256,1024]{1,0:T(8,128)S(1)} %constant_dynamic-update-slice_fusion.refs_0_), channel_id=1, source_target_pairs={{0,64},{8,72},{16,80},{24,88},{32,96},{40,104},{48,112},{56,120},{... | collective-permute-start | bytes 3145736 | tf_op jit(solution)/shard_map/ppermute | solution.py:281
  24.4 26.8 %collective-permute-done.6 = f32[64,1024]{1,0:T(8,128)S(1)} collective-permute-done((f32[64,1024]{1,0:T(8,128)S(1)}, f32[64,1024]{1,0:T(8,128)S(1)}, u32[]{:S(2)}, u32[]{:S(2)}) %collective-permute-start.6) | collective-permute-done | bytes 262176 | tf_op jit(solution)/shard_map/ppermute | solution.py:281
  52.2 2.4 collective-permute-start.8
  54.6 2.7 collective-permute-start.10
  57.2 9.2 %collective-permute-done.7.refs_1_ = f32[128,1024]{1,0:T(8,128)S(1)} collective-permute-done((f32[128,1024]{1,0:T(8,128)}, f32[128,1024]{1,0:T(8,128)S(1)}, u32[]{:S(2)}, u32[]{:S(2)}) %collective-permute-start.7) | collective-permute-done | bytes 524320 | tf_op jit(solution)/shard_map/ppermute | solution.py:281
  66.4 12.5 %collective-permute-start.4 = (f32[256,1024]{1,0:T(8,128)S(1)}, f32[256,1024]{1,0:T(8,128)}, u32[]{:S(2)}, u32[]{:S(2)}) collective-permute-start(f32[256,1024]{1,0:T(8,128)S(1)} %constant_dynamic-update-slice_fusion.refs_0_), channel_id=1, source_target_pairs={{0,8},{8,0},{16,24},{24,16},{32,40},{40,32},{48,56},{56,48},{64,72... | collective-permute-start | bytes 3145736 | tf_op jit(solution)/shard_map/ppermute | solution.py:281
  79.0 2.2 copy.27
  81.3 1.5 reshape.67.refs_9_.site_matrix_ref
  86.1 0.7 collective-permute-done.13.refs_7_
  86.9 0.8 copy-done.7
  87.6 16.3 %back.1 = (bf16[1024,1024]{1,0:T(8,128)(2,1)}, bf16[1024,1024]{1,0:T(8,128)(2,1)}, bf16[1024,1024]{1,0:T(8,128)(2,1)}, bf16[1024,1024]{1,0:T(8,128)(2,1)}, bf16[...) custom-call(s32[16]{0:T(128)} %get-tuple-element.70.offsets_ref, ...), custom_call_target="tpu_custom_call" | custom-call | tf_op jit(solution)/shard_map/back/pallas_call | solution.py:198
  104.0 13.9 %edge.1 = (bf16[1024,1024]{1,0:T(8,128)(2,1)}, bf16[1024,1024]{1,0:T(8,128)(2,1)}, f32[2,2,64,1024]{3,2,1,0:T(8,128)}, f32[2,2,64,1024]{3,2,1,0:T(8,128)}, f32[4,2,64,1024]{3,2,1,0:T(8,128)}) custom-call(s32[16]{0:T(128)} %get-tuple-element.71.offsets_ref, s32[8]{0:T(128)} %and_add_fusion.sources_ref, f32[256,1024]{1,0:T(8,128)} %copy-done.3, ...), custom_call_target="tpu_custom_call" | custom-call | tf_op jit(solution)/shard_map/edge/pallas_call | solution.py:218
  118.0 31.5 %left.1 = (f32[2,2,64,1024]{3,2,1,0:T(8,128)}, f32[2,2,64,1024]{3,2,1,0:T(8,128)}, f32[4,2,64,1024]{3,2,1,0:T(8,128)}, f32[256,256]{1,0:T(8,128)}) custom-call(s32[8]{0:T(128)} %and_add_fusion.sources_ref, f32[1024,1024]{1,0:T(8,128)} %bitcast.75, bf16[1024,1024]{1,0:T(8,128)(2,1)} %get-tuple-element.36.right_high_ref, ...), custom_call_target="tpu_custom_call" | custom-call | tf_op jit(solution)/shard_map/left/pallas_call | solution.py:238
  149.5 0.9 dynamic-slice_bitcast_fusion
  150.8 1.0 collective-permute-done.19
  151.8 0.9 bitcast_add_fusion
  152.8 2.8 collective-permute-start.20
  155.5 1.9 collective-permute-done.20
  157.6 1.5 collective-permute-start.21
  159.0 1.1 collective-permute-done.23
  160.1 1.3 collective-permute-done.21
  161.4 1.7 collective-permute-done.22
  163.1 2.6 collective-permute-start.26
  165.7 1.7 collective-permute-start.25
  167.4 2.1 collective-permute-done.24
  169.8 0.7 collective-permute-start.27
  170.5 13.0 %right.1 = (f32[512,1024]{1,0:T(8,128)}, f32[512,1024]{1,0:T(8,128)}) custom-call(s32[16]{0:T(128)} %get-tuple-element.69.places_ref, bf16[1024,1024]{1,0:T(8,128)(2,1)} %get-tuple-element.31.refs_4_.back_high_ref, bf16[1024,1024]{1,0:T(8,128)(2,1)} %get-tuple-element.32.refs_5_.back_low_ref, f32[1024,1024]{1,0:T(8,128)} %bitcast.76), custom_call_target="tpu_custom_call" | custom-call | tf_op jit(solution)/shard_map/right/pallas_call | solution.py:261
  183.5 4.9 %collective-permute-start.38 = (f32[512,1024]{1,0:T(8,128)}, f32[512,1024]{1,0:T(8,128)}, u32[]{:S(2)}, u32[]{:S(2)}) collective-permute-start(f32[512,1024]{1,0:T(8,128)} %get-tuple-element.47), channel_id=1, source_target_pairs={{0,8},{8,0},{16,24},{24,16},{32,40},{40,32},{48,56},{56,48},{64,72... | collective-permute-start | bytes 6291464 | tf_op jit(solution)/shard_map/ppermute | solution.py:281
  188.5 1.1 collective-permute-start.28
  190.0 2.5 collective-permute-start.14
  193.2 3.3 %collective-permute-done.29 = f32[16,256]{1,0:T(8,128)S(1)} collective-permute-done((f32[16,256]{1,0:T(8,128)S(1)}, f32[16,256]{1,0:T(8,128)S(1)}, u32[]{:S(2)}, u32[]{:S(2)}) %collective-permute-start.29) | collective-permute-done | bytes 16416 | tf_op jit(solution)/shard_map/ppermute | solution.py:281
  197.3 3.4 %collective-permute-start.31 = (f32[64,256]{1,0:T(8,128)S(1)}, f32[64,256]{1,0:T(8,128)S(1)}, u32[]{:S(2)}, u32[]{:S(2)}) collective-permute-start(f32[64,256]{1,0:T(8,128)S(1)} %constant_dynamic-slice_fusion), channel_id=1, source_target_pairs={{0,64},{8,72},{16,80},{24,88},{32,96},{40,104},{48,112},{56,120},{... | collective-permute-start | bytes 196616 | tf_op jit(solution)/shard_map/ppermute | solution.py:281
  200.6 1.7 collective-permute-done.31
  202.3 2.5 collective-permute-start.32
  204.9 1.0 collective-permute-done.32
  205.8 1.7 collective-permute-start.33
  208.3 2.6 copy.29
  210.9 5.2 %collective-permute-done.15 = f32[2,2,64,1024]{3,2,1,0:T(8,128)} collective-permute-done((f32[2,2,64,1024]{3,2,1,0:T(8,128)}, f32[2,2,64,1024]{3,2,1,0:T(8,128)}, u32[]{:S(2)}, u32[]{:S(2)}) %collective-permute-start.15) | collective-permute-done | bytes 1048608 | tf_op jit(solution)/shard_map/ppermute | solution.py:285
  216.0 1.5 fusion.11
  217.5 2.4 collective-permute-start.17
  219.9 2.0 add.228
  222.8 15.8 %collective-permute-done.34 = f32[2,2,64,1024]{3,2,1,0:T(8,128)} collective-permute-done((f32[2,2,64,1024]{3,2,1,0:T(8,128)}, f32[2,2,64,1024]{3,2,1,0:T(8,128)}, u32[]{:S(2)}, u32[]{:S(2)}) %collective-permute-start.34) | collective-permute-done | bytes 1048608 | tf_op jit(solution)/shard_map/ppermute | solution.py:285
  239.0 2.2 collective-permute-start.40
  241.2 1.4 fusion.3
  242.6 6.1 %collective-permute-done.17 = f32[2,64,1024]{2,1,0:T(8,128)S(1)} collective-permute-done((f32[2,64,1024]{2,1,0:T(8,128)S(1)}, f32[2,64,1024]{2,1,0:T(8,128)S(1)}, u32[]{:S(2)}, u32[]{:S(2)}) %collective-permute-start.17) | collective-permute-done | bytes 524320 | tf_op jit(solution)/shard_map/ppermute | solution.py:285
  248.6 3.4 %collective-permute-start.36 = (f32[2,64,1024]{2,1,0:T(8,128)S(1)}, f32[2,64,1024]{2,1,0:T(8,128)S(1)}, u32[]{:S(2)}, u32[]{:S(2)}) collective-permute-start(f32[2,64,1024]{2,1,0:T(8,128)S(1)} %get-tuple-element.63), channel_id=1, source_target_pairs={{0,3},{1,0},{2,1},{3,2},{4,7},{5,4},{6,5},{7,6},{8,11},{9,8},{10,9... | collective-permute-start | bytes 1572872 | tf_op jit(solution)/shard_map/ppermute | solution.py:285
  252.0 1.2 fusion.10
  253.6 0.8 collective-permute-start.18
  254.6 2.8 collective-permute-start.42
  257.4 4.8 %collective-permute-done.36 = f32[2,64,1024]{2,1,0:T(8,128)S(1)} collective-permute-done((f32[2,64,1024]{2,1,0:T(8,128)S(1)}, f32[2,64,1024]{2,1,0:T(8,128)S(1)}, u32[]{:S(2)}, u32[]{:S(2)}) %collective-permute-start.36) | collective-permute-done | bytes 524320 | tf_op jit(solution)/shard_map/ppermute | solution.py:285
  262.2 1.2 fusion.2
  263.4 0.8 collective-permute-start.37
  264.2 9.1 %collective-permute-done.42 = f32[64,1024]{1,0:T(8,128)S(1)} collective-permute-done((f32[64,1024]{1,0:T(8,128)S(1)}, f32[64,1024]{1,0:T(8,128)S(1)}, u32[]{:S(2)}, u32[]{:S(2)}) %collective-permute-start.42) | collective-permute-done | bytes 262176 | tf_op jit(solution)/shard_map/ppermute | solution.py:281
  273.3 0.9 reshape.73
  274.4 1.2 copy.28
  275.6 7.0 %collective-permute-done.37 = f32[2,64,1024]{2,1,0:T(8,128)S(1)} collective-permute-done((f32[2,64,1024]{2,1,0:T(8,128)S(1)}, f32[2,64,1024]{2,1,0:T(8,128)S(1)}, u32[]{:S(2)}, u32[]{:S(2)}) %collective-permute-start.37) | collective-permute-done | bytes 524320 | tf_op jit(solution)/shard_map/ppermute | solution.py:285
  282.6 1.2 fusion.7
  283.8 1.2 copy.30
  (110 shorter events, 12.2 us)
Async XLA Ops:
  0.6 2.1 copy-start.8
  3.7 9.5 %collective-permute-start = (f32[64,1024]{1,0:T(8,128)S(1)}, f32[64,1024]{1,0:T(8,128)S(1)}, u32[]{:S(2)}, u32[]{:S(2)}) collective-permute-start(f32[64,1024]{1,0:T(8,128)S(1)} %reshape.66), channel_id=1, source_target_pairs={{0,16},{8,24},{16,32},{24,40},{32,48},{40,56},{48,0},{56,8},{64,80... | collective-permute-start | bytes 786440 | tf_op jit(solution)/shard_map/ppermute | solution.py:281
  5.9 7.4 %collective-permute-start.1 = (f32[64,1024]{1,0:T(8,128)S(1)}, f32[64,1024]{1,0:T(8,128)S(1)}, u32[]{:S(2)}, u32[]{:S(2)}) collective-permute-start(f32[64,1024]{1,0:T(8,128)S(1)} %reshape.66), channel_id=1, source_target_pairs={{0,48},{8,56},{16,0},{24,8},{32,16},{40,24},{48,32},{56,40},{64,11... | collective-permute-start | bytes 786440 | tf_op jit(solution)/shard_map/ppermute | solution.py:281
  7.4 12.4 %collective-permute-start.2 = (f32[64,1024]{1,0:T(8,128)S(1)}, f32[64,1024]{1,0:T(8,128)S(1)}, u32[]{:S(2)}, u32[]{:S(2)}) collective-permute-start(f32[64,1024]{1,0:T(8,128)S(1)} %reshape.66), channel_id=1, source_target_pairs={{0,32},{8,40},{16,48},{24,56},{32,0},{40,8},{48,16},{56,24},{64,96... | collective-permute-start | bytes 786440 | tf_op jit(solution)/shard_map/ppermute | solution.py:281
  19.9 61.3 %copy-start.3 = (f32[256,1024]{1,0:T(8,128)}, f32[256,1024]{1,0:T(8,128)S(1)}, u32[]{:S(2)}) copy-start(f32[256,1024]{1,0:T(8,128)S(1)} %constant_dynamic-update-slice_fusion.refs_0_) | copy-start | bytes 3145732
  19.9 59.0 %collective-permute-start.3 = (f32[256,1024]{1,0:T(8,128)S(1)}, f32[256,1024]{1,0:T(8,128)}, u32[]{:S(2)}, u32[]{:S(2)}) collective-permute-start(f32[256,1024]{1,0:T(8,128)S(1)} %constant_dynamic-update-slice_fusion.refs_0_), channel_id=1, source_target_pairs={{0,64},{8,72},{16,80},{24,88},{32,96},{40,104},{48,112},{56,120},{... | collective-permute-start | bytes 3145736 | tf_op jit(solution)/shard_map/ppermute | solution.py:281
  23.5 27.6 %collective-permute-start.6 = (f32[64,1024]{1,0:T(8,128)S(1)}, f32[64,1024]{1,0:T(8,128)S(1)}, u32[]{:S(2)}, u32[]{:S(2)}) collective-permute-start(f32[64,1024]{1,0:T(8,128)S(1)} %reshape.64), channel_id=1, source_target_pairs={{0,64},{8,72},{16,80},{24,88},{32,96},{40,104},{48,112},{56,120},{... | collective-permute-start | bytes 786440 | tf_op jit(solution)/shard_map/ppermute | solution.py:281
  51.9 14.5 %collective-permute-start.7 = (f32[128,1024]{1,0:T(8,128)}, f32[128,1024]{1,0:T(8,128)S(1)}, u32[]{:S(2)}, u32[]{:S(2)}) collective-permute-start(f32[128,1024]{1,0:T(8,128)} %constant_dynamic-update-slice_fusion.4.refs_0_), channel_id=1, source_target_pairs={{0,16},{8,24},{16,32},{24,40},{32,48},{40,56},{48,0},{56,8},{64,80... | collective-permute-start | bytes 1572872 | tf_op jit(solution)/shard_map/ppermute | solution.py:281
  52.2 30.7 %collective-permute-start.8 = (f32[128,1024]{1,0:T(8,128)}, f32[128,1024]{1,0:T(8,128)}, u32[]{:S(2)}, u32[]{:S(2)}) collective-permute-start(f32[128,1024]{1,0:T(8,128)} %constant_dynamic-update-slice_fusion.4.refs_0_), channel_id=1, source_target_pairs={{0,48},{8,56},{16,0},{24,8},{32,16},{40,24},{48,32},{56,40},{64,11... | collective-permute-start | bytes 1572872 | tf_op jit(solution)/shard_map/ppermute | solution.py:281
  54.6 29.0 %collective-permute-start.9 = (f32[128,1024]{1,0:T(8,128)}, f32[128,1024]{1,0:T(8,128)}, u32[]{:S(2)}, u32[]{:S(2)}) collective-permute-start(f32[128,1024]{1,0:T(8,128)} %constant_dynamic-update-slice_fusion.4.refs_0_), channel_id=1, source_target_pairs={{0,32},{8,40},{16,48},{24,56},{32,0},{40,8},{48,16},{56,24},{64,96... | collective-permute-start | bytes 1572872 | tf_op jit(solution)/shard_map/ppermute | solution.py:281
  54.6 29.1 %collective-permute-start.10 = (f32[128,1024]{1,0:T(8,128)}, f32[128,1024]{1,0:T(8,128)}, u32[]{:S(2)}, u32[]{:S(2)}) collective-permute-start(f32[128,1024]{1,0:T(8,128)} %constant_dynamic-update-slice_fusion.4.refs_0_), channel_id=1, source_target_pairs={{0,8},{8,0},{16,24},{24,16},{32,40},{40,32},{48,56},{56,48},{64,72... | collective-permute-start | bytes 1572872 | tf_op jit(solution)/shard_map/ppermute | solution.py:281
  66.4 12.6 %copy-start.4 = (f32[128,1024]{1,0:T(8,128)}, f32[128,1024]{1,0:T(8,128)S(1)}, u32[]{:S(2)}) copy-start(f32[128,1024]{1,0:T(8,128)S(1)} %collective-permute-done.7.refs_1_) | copy-start | bytes 1572868
  66.4 37.6 %collective-permute-start.4 = (f32[256,1024]{1,0:T(8,128)S(1)}, f32[256,1024]{1,0:T(8,128)}, u32[]{:S(2)}, u32[]{:S(2)}) collective-permute-start(f32[256,1024]{1,0:T(8,128)S(1)} %constant_dynamic-update-slice_fusion.refs_0_), channel_id=1, source_target_pairs={{0,8},{8,0},{16,24},{24,16},{32,40},{40,32},{48,56},{56,48},{64,72... | collective-permute-start | bytes 3145736 | tf_op jit(solution)/shard_map/ppermute | solution.py:281
  78.9 25.1 %collective-permute-start.5 = (f32[256,1024]{1,0:T(8,128)}, f32[256,1024]{1,0:T(8,128)}, u32[]{:S(2)}, u32[]{:S(2)}) collective-permute-start(f32[256,1024]{1,0:T(8,128)} %collective-permute-done.3.refs_1_), channel_id=1, source_target_pairs={{0,8},{8,0},{16,24},{24,16},{32,40},{40,32},{48,56},{56,48},{64,72... | collective-permute-start | bytes 3145736 | tf_op jit(solution)/shard_map/ppermute | solution.py:281
  81.2 2.9 %copy-start.9 = (s32[8]{0:T(128)S(1)}, s32[8]{0:T(128)}, u32[]{:S(2)}) copy-start(s32[8]{0:T(128)} %constant.77.clone) | copy-start | bytes 100
  81.2 2.9 %copy-start.10 = (s32[8]{0:T(128)S(1)}, s32[8]{0:T(128)}, u32[]{:S(2)}) copy-start(s32[8]{0:T(128)} %constant.76.clone) | copy-start | bytes 100
  81.2 3.5 %copy-start.11 = (s32[16]{0:T(128)S(1)}, s32[16]{0:T(128)}, u32[]{:S(2)}) copy-start(s32[16]{0:T(128)} %constant.73.clone) | copy-start | bytes 196
  81.2 3.4 %copy-start.12 = (s32[16]{0:T(128)S(1)}, s32[16]{0:T(128)}, u32[]{:S(2)}) copy-start(s32[16]{0:T(128)} %constant.81.clone) | copy-start | bytes 196
  81.3 3.4 %copy-start.13 = (s32[16]{0:T(128)S(1)}, s32[16]{0:T(128)}, u32[]{:S(2)}) copy-start(s32[16]{0:T(128)} %constant.80.clone) | copy-start | bytes 196
  81.3 3.4 %copy-start.14 = (s32[16]{0:T(128)S(1)}, s32[16]{0:T(128)}, u32[]{:S(2)}) copy-start(s32[16]{0:T(128)} %constant.75.clone) | copy-start | bytes 196
  81.3 3.4 %copy-start.15 = (s32[16]{0:T(128)S(1)}, s32[16]{0:T(128)}, u32[]{:S(2)}) copy-start(s32[16]{0:T(128)} %constant.83) | copy-start | bytes 196
  81.3 3.4 %copy-start.16 = (s32[16]{0:T(128)S(1)}, s32[16]{0:T(128)}, u32[]{:S(2)}) copy-start(s32[16]{0:T(128)} %constant.82) | copy-start | bytes 196
  81.3 3.4 %copy-start.17 = (s32[16]{0:T(128)S(1)}, s32[16]{0:T(128)}, u32[]{:S(2)}) copy-start(s32[16]{0:T(128)} %constant.78.clone) | copy-start | bytes 196
  82.9 2.5 collective-permute-start.11
  83.6 2.5 collective-permute-start.12
  83.7 3.2 %collective-permute-start.13 = (f32[128,1024]{1,0:T(8,128)}, f32[128,1024]{1,0:T(8,128)S(1)}, u32[]{:S(2)}, u32[]{:S(2)}) collective-permute-start(f32[128,1024]{1,0:T(8,128)} %collective-permute-done.9.refs_3_), channel_id=1, source_target_pairs={{0,8},{8,0},{16,24},{24,16},{32,40},{40,32},{48,56},{56,48},{64,72... | collective-permute-start | bytes 1572872 | tf_op jit(solution)/shard_map/ppermute | solution.py:281
  85.3 1.5 copy-start.5
  86.1 0.8 copy-start.6
  86.8 0.8 copy-start.7
  150.4 1.4 collective-permute-start.19
  152.8 4.7 %collective-permute-start.20 = (f32[64,256]{1,0:T(8,128)S(1)}, f32[64,256]{1,0:T(8,128)S(1)}, u32[]{:S(2)}, u32[]{:S(2)}) collective-permute-start(f32[64,256]{1,0:T(8,128)S(1)} %dynamic-slice_bitcast_fusion.1), channel_id=1, source_target_pairs={{0,64},{8,72},{16,80},{24,88},{32,96},{40,104},{48,112},{56,120},{... | collective-permute-start | bytes 196616 | tf_op jit(solution)/shard_map/ppermute | solution.py:281
  157.5 2.7 collective-permute-start.23
  157.6 3.9 %collective-permute-start.21 = (f32[16,256]{1,0:T(8,128)S(1)}, f32[16,256]{1,0:T(8,128)S(1)}, u32[]{:S(2)}, u32[]{:S(2)}) collective-permute-start(f32[16,256]{1,0:T(8,128)S(1)} %get-tuple-element.68), channel_id=1, source_target_pairs={{0,16},{8,24},{16,32},{24,40},{32,48},{40,56},{48,0},{56,8},{64,80... | collective-permute-start | bytes 49160 | tf_op jit(solution)/shard_map/ppermute | solution.py:281
  159.0 4.1 %collective-permute-start.22 = (f32[16,256]{1,0:T(8,128)S(1)}, f32[16,256]{1,0:T(8,128)S(1)}, u32[]{:S(2)}, u32[]{:S(2)}) collective-permute-start(f32[16,256]{1,0:T(8,128)S(1)} %get-tuple-element.66), channel_id=1, source_target_pairs={{0,32},{8,40},{16,48},{24,56},{32,0},{40,8},{48,16},{56,24},{64,96... | collective-permute-start | bytes 49160 | tf_op jit(solution)/shard_map/ppermute | solution.py:281
  163.1 4.3 %collective-permute-start.26 = (f32[16,256]{1,0:T(8,128)S(1)}, f32[16,256]{1,0:T(8,128)S(1)}, u32[]{:S(2)}, u32[]{:S(2)}) collective-permute-start(f32[16,256]{1,0:T(8,128)S(1)} %bitcast_add_fusion.2), channel_id=1, source_target_pairs={{0,3},{1,0},{2,1},{3,2},{4,7},{5,4},{6,5},{7,6},{8,11},{9,8},{10,9... | collective-permute-start | bytes 49160 | tf_op jit(solution)/shard_map/ppermute | solution.py:285
  165.7 3.8 %collective-permute-start.24 = (f32[16,256]{1,0:T(8,128)S(1)}, f32[16,256]{1,0:T(8,128)S(1)}, u32[]{:S(2)}, u32[]{:S(2)}) collective-permute-start(f32[16,256]{1,0:T(8,128)S(1)} %bitcast_add_fusion.2), channel_id=1, source_target_pairs={{0,1},{1,2},{2,3},{3,0},{4,5},{5,6},{6,7},{7,4},{8,9},{9,10},{10,1... | collective-permute-start | bytes 49160 | tf_op jit(solution)/shard_map/ppermute | solution.py:285
  165.7 4.1 %collective-permute-start.25 = (f32[16,256]{1,0:T(8,128)S(1)}, f32[16,256]{1,0:T(8,128)S(1)}, u32[]{:S(2)}, u32[]{:S(2)}) collective-permute-start(f32[16,256]{1,0:T(8,128)S(1)} %bitcast_add_fusion.2), channel_id=1, source_target_pairs={{0,2},{1,3},{2,0},{3,1},{4,6},{5,7},{6,4},{7,5},{8,10},{9,11},{10,... | collective-permute-start | bytes 49160 | tf_op jit(solution)/shard_map/ppermute | solution.py:285
  169.8 18.7 %collective-permute-start.27 = (f32[16,256]{1,0:T(8,128)S(1)}, f32[16,256]{1,0:T(8,128)S(1)}, u32[]{:S(2)}, u32[]{:S(2)}) collective-permute-start(f32[16,256]{1,0:T(8,128)S(1)} %add_add_fusion.1), channel_id=1, source_target_pairs={{0,4},{1,5},{2,6},{3,7},{4,0},{5,1},{6,2},{7,3},{8,12},{9,13},{10,... | collective-permute-start | bytes 49160 | tf_op jit(solution)/shard_map/ppermute | solution.py:285
  183.5 36.4 %collective-permute-start.38 = (f32[512,1024]{1,0:T(8,128)}, f32[512,1024]{1,0:T(8,128)}, u32[]{:S(2)}, u32[]{:S(2)}) collective-permute-start(f32[512,1024]{1,0:T(8,128)} %get-tuple-element.47), channel_id=1, source_target_pairs={{0,8},{8,0},{16,24},{24,16},{32,40},{40,32},{48,56},{56,48},{64,72... | collective-permute-start | bytes 6291464 | tf_op jit(solution)/shard_map/ppermute | solution.py:281
  188.5 4.5 %collective-permute-start.28 = (f32[16,256]{1,0:T(8,128)S(1)}, f32[16,256]{1,0:T(8,128)S(1)}, u32[]{:S(2)}, u32[]{:S(2)}) collective-permute-start(f32[16,256]{1,0:T(8,128)S(1)} %get-tuple-element.57), channel_id=1, source_target_pairs={{0,48},{8,56},{16,0},{24,8},{32,16},{40,24},{48,32},{56,40},{64,11... | collective-permute-start | bytes 49160 | tf_op jit(solution)/shard_map/ppermute | solution.py:281
  189.5 26.5 %collective-permute-start.15 = (f32[2,2,64,1024]{3,2,1,0:T(8,128)}, f32[2,2,64,1024]{3,2,1,0:T(8,128)}, u32[]{:S(2)}, u32[]{:S(2)}) collective-permute-start(f32[2,2,64,1024]{3,2,1,0:T(8,128)} %get-tuple-element.35), channel_id=1, source_target_pairs={{0,1},{1,2},{2,3},{3,0},{4,5},{5,6},{6,7},{7,4},{8,9},{9,10},{10,1... | collective-permute-start | bytes 3145736 | tf_op jit(solution)/shard_map/ppermute | solution.py:285
  190.0 26.0 %collective-permute-start.14 = (f32[2,2,64,1024]{3,2,1,0:T(8,128)}, f32[2,2,64,1024]{3,2,1,0:T(8,128)S(1)}, u32[]{:S(2)}, u32[]{:S(2)}) collective-permute-start(f32[2,2,64,1024]{3,2,1,0:T(8,128)} %get-tuple-element.34), channel_id=1, source_target_pairs={{0,3},{1,0},{2,1},{3,2},{4,7},{5,4},{6,5},{7,6},{8,11},{9,8},{10,9... | collective-permute-start | bytes 3145736 | tf_op jit(solution)/shard_map/ppermute | solution.py:285
  192.5 4.1 %collective-permute-start.29 = (f32[16,256]{1,0:T(8,128)S(1)}, f32[16,256]{1,0:T(8,128)S(1)}, u32[]{:S(2)}, u32[]{:S(2)}) collective-permute-start(f32[16,256]{1,0:T(8,128)S(1)} %get-tuple-element.57), channel_id=1, source_target_pairs={{0,32},{8,40},{16,48},{24,56},{32,0},{40,8},{48,16},{56,24},{64,96... | collective-permute-start | bytes 49160 | tf_op jit(solution)/shard_map/ppermute | solution.py:281
  193.0 4.2 %collective-permute-start.30 = (f32[16,256]{1,0:T(8,128)S(1)}, f32[16,256]{1,0:T(8,128)S(1)}, u32[]{:S(2)}, u32[]{:S(2)}) collective-permute-start(f32[16,256]{1,0:T(8,128)S(1)} %get-tuple-element.57), channel_id=1, source_target_pairs={{0,16},{8,24},{16,32},{24,40},{32,48},{40,56},{48,0},{56,8},{64,80... | collective-permute-start | bytes 49160 | tf_op jit(solution)/shard_map/ppermute | solution.py:281
  197.3 5.0 %collective-permute-start.31 = (f32[64,256]{1,0:T(8,128)S(1)}, f32[64,256]{1,0:T(8,128)S(1)}, u32[]{:S(2)}, u32[]{:S(2)}) collective-permute-start(f32[64,256]{1,0:T(8,128)S(1)} %constant_dynamic-slice_fusion), channel_id=1, source_target_pairs={{0,64},{8,72},{16,80},{24,88},{32,96},{40,104},{48,112},{56,120},{... | collective-permute-start | bytes 196616 | tf_op jit(solution)/shard_map/ppermute | solution.py:281
  202.3 3.5 %collective-permute-start.32 = (f32[128,256]{1,0:T(8,128)S(1)}, f32[128,256]{1,0:T(8,128)S(1)}, u32[]{:S(2)}, u32[]{:S(2)}) collective-permute-start(f32[128,256]{1,0:T(8,128)S(1)} %maximum_select_fusion.1), channel_id=1, source_target_pairs={{0,8},{8,0},{16,24},{24,16},{32,40},{40,32},{48,56},{56,48},{64,72... | collective-permute-start | bytes 393224 | tf_op jit(solution)/shard_map/ppermute | solution.py:281
  204.9 33.7 %collective-permute-start.34 = (f32[2,2,64,1024]{3,2,1,0:T(8,128)}, f32[2,2,64,1024]{3,2,1,0:T(8,128)}, u32[]{:S(2)}, u32[]{:S(2)}) collective-permute-start(f32[2,2,64,1024]{3,2,1,0:T(8,128)} %get-tuple-element.45), channel_id=1, source_target_pairs={{0,1},{1,2},{2,3},{3,0},{4,5},{5,6},{6,7},{7,4},{8,9},{9,10},{10,1... | collective-permute-start | bytes 3145736 | tf_op jit(solution)/shard_map/ppermute | solution.py:285
  205.8 33.1 %collective-permute-start.33 = (f32[2,2,64,1024]{3,2,1,0:T(8,128)}, f32[2,2,64,1024]{3,2,1,0:T(8,128)}, u32[]{:S(2)}, u32[]{:S(2)}) collective-permute-start(f32[2,2,64,1024]{3,2,1,0:T(8,128)} %get-tuple-element.44), channel_id=1, source_target_pairs={{0,3},{1,0},{2,1},{3,2},{4,7},{5,4},{6,5},{7,6},{8,11},{9,8},{10,9... | collective-permute-start | bytes 3145736 | tf_op jit(solution)/shard_map/ppermute | solution.py:285
  210.9 9.0 %copy-start = (f32[512,1024]{1,0:T(8,128)S(1)}, f32[512,1024]{1,0:T(8,128)}, u32[]{:S(2)}) copy-start(f32[512,1024]{1,0:T(8,128)} %get-tuple-element.46) | copy-start | bytes 6291460
  217.5 31.1 %collective-permute-start.17 = (f32[2,64,1024]{2,1,0:T(8,128)S(1)}, f32[2,64,1024]{2,1,0:T(8,128)S(1)}, u32[]{:S(2)}, u32[]{:S(2)}) collective-permute-start(f32[2,64,1024]{2,1,0:T(8,128)S(1)} %get-tuple-element.65), channel_id=1, source_target_pairs={{0,3},{1,0},{2,1},{3,2},{4,7},{5,4},{6,5},{7,6},{8,11},{9,8},{10,9... | collective-permute-start | bytes 1572872 | tf_op jit(solution)/shard_map/ppermute | solution.py:285
  219.9 54.3 %collective-permute-start.16 = (f32[2,64,1024]{2,1,0:T(8,128)S(1)}, f32[2,64,1024]{2,1,0:T(8,128)S(1)}, u32[]{:S(2)}, u32[]{:S(2)}) collective-permute-start(f32[2,64,1024]{2,1,0:T(8,128)S(1)} %get-tuple-element.64), channel_id=1, source_target_pairs={{0,1},{1,2},{2,3},{3,0},{4,5},{5,6},{6,7},{7,4},{8,9},{9,10},{10,1... | collective-permute-start | bytes 1572872 | tf_op jit(solution)/shard_map/ppermute | solution.py:285
  221.9 19.3 %copy-start.1 = (f32[4,2,64,1024]{3,2,1,0:T(8,128)S(1)}, f32[4,2,64,1024]{3,2,1,0:T(8,128)}, u32[]{:S(2)}) copy-start(f32[4,2,64,1024]{3,2,1,0:T(8,128)} %get-tuple-element.43) | copy-start | bytes 6291460
  222.2 29.9 %copy-start.2 = (f32[4,2,64,1024]{3,2,1,0:T(8,128)S(1)}, f32[4,2,64,1024]{3,2,1,0:T(8,128)}, u32[]{:S(2)}) copy-start(f32[4,2,64,1024]{3,2,1,0:T(8,128)} %get-tuple-element.33) | copy-start | bytes 6291460
  222.2 31.0 %collective-permute-start.41 = (f32[2,64,1024]{2,1,0:T(8,128)S(1)}, f32[2,64,1024]{2,1,0:T(8,128)S(1)}, u32[]{:S(2)}, u32[]{:S(2)}) collective-permute-start(f32[2,64,1024]{2,1,0:T(8,128)S(1)} %bitcast.89), channel_id=1, source_target_pairs={{0,32},{8,40},{16,48},{24,56},{32,0},{40,8},{48,16},{56,24},{64,96... | collective-permute-start | bytes 1572872 | tf_op jit(solution)/shard_map/ppermute | solution.py:281
  238.5 15.0 %collective-permute-start.39 = (f32[2,64,1024]{2,1,0:T(8,128)S(1)}, f32[2,64,1024]{2,1,0:T(8,128)S(1)}, u32[]{:S(2)}, u32[]{:S(2)}) collective-permute-start(f32[2,64,1024]{2,1,0:T(8,128)S(1)} %bitcast.88), channel_id=1, source_target_pairs={{0,16},{8,24},{16,32},{24,40},{32,48},{40,56},{48,0},{56,8},{64,80... | collective-permute-start | bytes 1572872 | tf_op jit(solution)/shard_map/ppermute | solution.py:281
  239.0 15.4 %collective-permute-start.40 = (f32[2,64,1024]{2,1,0:T(8,128)S(1)}, f32[2,64,1024]{2,1,0:T(8,128)S(1)}, u32[]{:S(2)}, u32[]{:S(2)}) collective-permute-start(f32[2,64,1024]{2,1,0:T(8,128)S(1)} %bitcast.87), channel_id=1, source_target_pairs={{0,48},{8,56},{16,0},{24,8},{32,16},{40,24},{48,32},{56,40},{64,11... | collective-permute-start | bytes 1572872 | tf_op jit(solution)/shard_map/ppermute | solution.py:281
  248.6 13.5 %collective-permute-start.36 = (f32[2,64,1024]{2,1,0:T(8,128)S(1)}, f32[2,64,1024]{2,1,0:T(8,128)S(1)}, u32[]{:S(2)}, u32[]{:S(2)}) collective-permute-start(f32[2,64,1024]{2,1,0:T(8,128)S(1)} %get-tuple-element.63), channel_id=1, source_target_pairs={{0,3},{1,0},{2,1},{3,2},{4,7},{5,4},{6,5},{7,6},{8,11},{9,8},{10,9... | collective-permute-start | bytes 1572872 | tf_op jit(solution)/shard_map/ppermute | solution.py:285
  253.2 22.4 %collective-permute-start.35 = (f32[2,64,1024]{2,1,0:T(8,128)S(1)}, f32[2,64,1024]{2,1,0:T(8,128)S(1)}, u32[]{:S(2)}, u32[]{:S(2)}) collective-permute-start(f32[2,64,1024]{2,1,0:T(8,128)S(1)} %get-tuple-element.62), channel_id=1, source_target_pairs={{0,1},{1,2},{2,3},{3,0},{4,5},{5,6},{6,7},{7,4},{8,9},{9,10},{10,1... | collective-permute-start | bytes 1572872 | tf_op jit(solution)/shard_map/ppermute | solution.py:285
  253.6 20.7 %collective-permute-start.18 = (f32[2,64,1024]{2,1,0:T(8,128)S(1)}, f32[2,64,1024]{2,1,0:T(8,128)S(1)}, u32[]{:S(2)}, u32[]{:S(2)}) collective-permute-start(f32[2,64,1024]{2,1,0:T(8,128)S(1)} %fusion.10), channel_id=1, source_target_pairs={{0,4},{1,5},{2,6},{3,7},{4,0},{5,1},{6,2},{7,3},{8,12},{9,13},{10,... | collective-permute-start | bytes 1572872 | tf_op jit(solution)/shard_map/ppermute | solution.py:285
  254.6 18.7 %collective-permute-start.42 = (f32[64,1024]{1,0:T(8,128)S(1)}, f32[64,1024]{1,0:T(8,128)S(1)}, u32[]{:S(2)}, u32[]{:S(2)}) collective-permute-start(f32[64,1024]{1,0:T(8,128)S(1)} %slice_bitcast_fusion), channel_id=1, source_target_pairs={{0,64},{8,72},{16,80},{24,88},{32,96},{40,104},{48,112},{56,120},{... | collective-permute-start | bytes 786440 | tf_op jit(solution)/shard_map/ppermute | solution.py:281
  263.4 19.2 %collective-permute-start.37 = (f32[2,64,1024]{2,1,0:T(8,128)S(1)}, f32[2,64,1024]{2,1,0:T(8,128)S(1)}, u32[]{:S(2)}, u32[]{:S(2)}) collective-permute-start(f32[2,64,1024]{2,1,0:T(8,128)S(1)} %fusion.2), channel_id=1, source_target_pairs={{0,4},{1,5},{2,6},{3,7},{4,0},{5,1},{6,2},{7,3},{8,12},{9,13},{10,... | collective-permute-start | bytes 1572872 | tf_op jit(solution)/shard_map/ppermute | solution.py:285
